TPU v7x, 32 devices: a whole 2x2x4 slice. The times are simulated.
32 devices in a mesh: wide: 16 (over z, y, core), narrow: 2 (over x).
Axes of the slice: x: 2, y: 2, z: 4, core: 2. Of those that a mesh axis runs over, the one named last changes fastest.
Arguments:
- tokens: bfloat16 [32, 256, 1120], P(('wide', 'narrow')), may hold values from -6 to 6
- lengths: int32 [32], P(('wide', 'narrow')), may hold values from 128 to 256
- dropped: int32 [32], P(('wide', 'narrow')), may hold values from 0 to 4
- cotangent: bfloat16 [32, 256, 1120], P(('wide', 'narrow')), may hold values from -6 to 6
- first_gain: bfloat16 [1120], P('narrow'), may hold values from 0.5 to 1.5
- first_shift: bfloat16 [1120], P('narrow'), may hold values from -1.5 to 1.5
- qkv_weight: bfloat16 [1120, 3360], P('narrow'), may hold values from -0.1875 to 0.1875
- query_bias: bfloat16 [1120], P('narrow'), may hold values from -2 to 2
- value_bias: bfloat16 [1120], P('narrow'), may hold values from -2 to 2
- out_weight: bfloat16 [1120, 1120], P('narrow'), may hold values from -1.5 to 1.5
- out_bias: bfloat16 [1120], P('narrow'), may hold values from -1.5 to 1.5
- second_gain: bfloat16 [1120], P('narrow'), may hold values from 0.5 to 1.5
- second_shift: bfloat16 [1120], P('narrow'), may hold values from -1.5 to 1.5
- up_weight: bfloat16 [1120, 4480], P('narrow'), may hold values from -0.1875 to 0.1875
- up_bias: bfloat16 [4480], P('narrow'), may hold values from -2 to 2
- down_weight: bfloat16 [4480, 1120], P('narrow'), may hold values from -0.1875 to 0.1875
- down_bias: bfloat16 [1120], P('narrow'), may hold values from -1.5 to 1.5
Outputs:
- output: bfloat16 [32, 256, 1120], P(('wide', 'narrow'))
- grad_tokens: float32 [32, 256, 1120], P(('wide', 'narrow'))
- grad_first_gain: float32 [1120], P('narrow')
- grad_first_shift: float32 [1120], P('narrow')
- grad_qkv_weight: float32 [1120, 3360], P('narrow', 'wide')
- grad_query_bias: float32 [1120], P('narrow')
- grad_value_bias: float32 [1120], P('narrow')
- grad_out_weight: float32 [1120, 1120], P('narrow', 'wide')
- grad_out_bias: float32 [1120], P('narrow')
- grad_second_gain: float32 [1120], P('narrow')
- grad_second_shift: float32 [1120], P('narrow')
- grad_up_weight: float32 [1120, 4480], P('narrow', 'wide')
- grad_up_bias: float32 [4480], P('narrow')
- grad_down_weight: float32 [4480, 1120], P('narrow', 'wide')
- grad_down_bias: float32 [1120], P('narrow')
All inputs are finite; a program needn't handle non-finite values.
Results may differ from a plain program's by a relative error of at most 0.018.
Values may be sent and summed in bfloat16 or wider, within the bound.
A program may use at most 192 MiB of HBM per device.

v0:
```python
import jax
import jax.numpy as jnp
from jax import lax
from jax.sharding import PartitionSpec as P

HEAD = 56
epsilon = 1e-05
head_groups = 4
AXES = ("wide", "narrow")
f32 = jnp.float32
bf16 = jnp.bfloat16


def dot(left, right):
    return jnp.dot(left, right, preferred_element_type=f32)


def tdot(left, right):
    return lax.dot_general(left, right, (((0,), (0,)), ((), ())), preferred_element_type=f32)


def dot_t(left, right):
    return lax.dot_general(left, right, (((1,), (1,)), ((), ())), preferred_element_type=f32)


def normed(values, gain, shift):
    center = values - jnp.mean(values, axis=-1, keepdims=True)
    spread = jnp.mean(center * center, axis=-1, keepdims=True)
    return center * lax.rsqrt(spread + epsilon) * gain + shift


def split_heads(matrix):
    rows = matrix.shape[0]
    return matrix.reshape(rows, head_groups, -1, HEAD).transpose(1, 0, 2, 3)


def join_heads(blocks):
    return blocks.transpose(1, 0, 2, 3).reshape(blocks.shape[1], -1)


def key_mask(length, drop, rows):
    places = jnp.arange(rows, dtype=jnp.int32)
    live = (places < length) & ((places < 1) | (places > drop))
    return (places[None, :] <= places[:, None]) & (
        live[None, :] | (places[None, :] == places[:, None])
    )


def scores_of(query, keys, mask):
    raw = jnp.einsum("qhe,khe->hqk", query, keys, preferred_element_type=f32) * HEAD ** (-0.5)
    return jnp.where(mask[None], raw, -jnp.inf)


def attention(query, keys, values, mask):

    def attend(group):
        scores = scores_of(group[0], group[1], mask)
        top = jnp.max(scores, axis=-1, keepdims=True)
        expos = jnp.exp(scores - top)
        total = jnp.sum(expos, axis=-1, keepdims=True)
        probs = (expos / total).astype(bf16)
        heads_out = jnp.einsum("hqk,khe->qhe", probs, group[2], preferred_element_type=f32)
        return (heads_out.astype(bf16), top + jnp.log(total))

    heads_out, logsum = lax.map(
        attend, (split_heads(query), split_heads(keys), split_heads(values))
    )
    return (join_heads(heads_out), logsum)


def attention_back(query, keys, values, logsum, d_attended, mask):

    def attend_back(group):
        q_part, k_part, v_part, lse_part, do_part = group
        scores = scores_of(q_part, k_part, mask)
        probs = jnp.exp(scores - lse_part)
        rounded = probs.astype(bf16)
        d_v = jnp.einsum("hqk,qhe->khe", rounded, do_part, preferred_element_type=f32)
        d_probs = jnp.einsum("qhe,khe->hqk", do_part, v_part, preferred_element_type=f32)
        inner = jnp.sum(d_probs * probs, axis=-1, keepdims=True)
        d_scores = (probs * (d_probs - inner)).astype(bf16)
        d_q = jnp.einsum("hqk,khe->qhe", d_scores, k_part, preferred_element_type=f32)
        d_k = jnp.einsum("hqk,qhe->khe", d_scores, q_part, preferred_element_type=f32)
        d_q = d_q * HEAD ** (-0.5)
        d_k = d_k * HEAD ** (-0.5)
        return (d_q.astype(bf16), d_k.astype(bf16), d_v.astype(bf16))

    d_qs, d_ks, d_vs = lax.map(
        attend_back,
        (
            split_heads(query),
            split_heads(keys),
            split_heads(values),
            logsum,
            split_heads(d_attended),
        ),
    )
    return (join_heads(d_qs), join_heads(d_ks), join_heads(d_vs))


class Links:

    def __init__(self):
        self.count = lax.axis_size("narrow")
        self.wide = lax.axis_size("wide")
        self.x = lax.axis_index("narrow")
        spot = lax.axis_index("wide")
        self.core = spot % 2
        self.y = spot // 2 % 2
        self.z = spot // 4
        self.depth = self.wide // 4
        self.direct = self.count == 2 and self.wide == 16

    def table(self, move):
        pairs = []
        for i in range(self.count * self.wide):
            x = i % self.count
            spot = i // self.count
            to = move(x, spot // 2 % 2, spot // 4, spot % 2)
            if to is not None:
                pairs.append((i, ((to[2] * 2 + to[1]) * 2 + to[3]) * self.count + to[0]))
        return pairs

    def send(self, value, move):
        return lax.ppermute(value, AXES, self.table(move))

    def over_x(self, value):
        return self.send(value, lambda x, y, z, c: (1 - x, y, z, c))

    def over_y(self, value):
        return self.send(value, lambda x, y, z, c: (x, 1 - y, z, c))

    def over_core(self, value):
        return self.send(value, lambda x, y, z, c: (x, y, z, 1 - c))


def pick(which, zero, one):
    return jnp.where(which == 0, zero, one)


def gather_other(links, shard):
    rows, columns = shard.shape
    tiles = rows // 8
    span = -(-tiles // 4)
    starts = [tiles * k // 4 for k in range(4)]
    view = shard.reshape(tiles, 8, columns)
    start_of = jnp.array(starts, jnp.int32)
    mine = links.y * 2 + links.core

    def at(y, core):
        return start_of[y * 2 + core]

    piece = lax.dynamic_slice_in_dim(view, start_of[mine], span, 0)
    first = links.over_x(piece)
    second = links.over_y(first)
    third = links.over_core(first)
    fourth = links.over_core(second)
    whole = jnp.zeros((tiles, 8, columns), shard.dtype)
    y, core = (links.y, links.core)
    for value, spot in (
        (first, at(y, core)),
        (second, at(1 - y, core)),
        (third, at(y, 1 - core)),
        (fourth, at(1 - y, 1 - core)),
    ):
        whole = lax.dynamic_update_slice_in_dim(whole, value, spot, 0)
    return whole.reshape(rows, columns)


class Weight:

    def __init__(self, links, shard):
        self.links = links
        self.own = shard
        if links.direct:
            self.other = gather_other(links, shard)
        else:
            self.full = lax.all_gather(shard, "narrow", axis=0, tiled=True)

    def apply(self, left):
        if not self.links.direct:
            return dot(left, self.full)
        x = self.links.x
        half = left.shape[1] // 2
        mine = pick(x, left[:, :half], left[:, half:])
        theirs = pick(x, left[:, half:], left[:, :half])
        return dot(mine, self.own) + dot(theirs, self.other)

    def apply_t(self, left):
        if not self.links.direct:
            return dot_t(left, self.full)
        x = self.links.x
        mine = dot_t(left, self.own)
        theirs = dot_t(left, self.other)
        return jnp.concatenate([pick(x, mine, theirs), pick(x, theirs, mine)], axis=1)


def weight_grad(links, left, right):
    if not links.direct:
        grad = tdot(left, right).astype(bf16)
        grad = lax.psum_scatter(grad, "narrow", scatter_dimension=0, tiled=True)
        return lax.psum_scatter(grad, "wide", scatter_dimension=1, tiled=True).astype(f32)
    x, y, z, core = (links.x, links.y, links.z, links.core)
    rows, columns = (left.shape[1], right.shape[1])
    half = rows // 2
    unit = columns // 8
    right_own = pick(core, right[:, : columns // 2], right[:, columns // 2 :])
    right_away = pick(core, right[:, columns // 2 :], right[:, : columns // 2])
    right_all = jnp.concatenate([right_own, links.over_core(right_away)], axis=0)
    left_all = jnp.concatenate([left, links.over_core(left)], axis=0)
    left_own = pick(x, left_all[:, :half], left_all[:, half:])
    left_away = pick(x, left_all[:, half:], left_all[:, :half])
    cut = [right_all[:, k * unit : (k + 1) * unit] for k in range(4)]
    near = [pick(y, cut[0], cut[1]), pick(y, cut[2], cut[3])]
    far = [pick(y, cut[1], cut[0]), pick(y, cut[3], cut[2])]

    def both(one, two):
        return jnp.stack([one.astype(bf16), two.astype(bf16)])

    got_x = links.over_x(both(tdot(far[0], left_away), tdot(near[0], left_away)))
    got_y = links.over_y(both(tdot(far[1], left_away), tdot(far[1], left_own)))
    sum_far = tdot(far[0], left_own) + got_x[0].astype(f32)
    even = tdot(near[0], left_own) + got_x[1].astype(f32)
    sum_away = tdot(near[1], left_away) + got_y[0].astype(f32)
    odd = tdot(near[1], left_own) + got_y[1].astype(f32)
    even = even + links.over_y(sum_far.astype(bf16)).astype(f32)
    odd = odd + links.over_x(sum_away.astype(bf16)).astype(f32)
    low = z % 2 == 0
    even_b, odd_b = (even.astype(bf16), odd.astype(bf16))
    same = jnp.where(low, odd_b, even_b)
    straight = jnp.where(low, even_b, odd_b)
    got_1 = links.send(same, lambda x, y, z, c: (x, y, z ^ 1, c) if z // 2 == c else None)
    got_2 = links.send(straight, lambda x, y, z, c: (x, y, z ^ 2, c) if z // 2 != c else None)
    got_3 = links.send(same, lambda x, y, z, c: (x, y, z ^ 3, c) if z // 2 != c else None)
    total = jnp.where(low, even, odd)
    total = total + got_1.astype(f32) + got_2.astype(f32) + got_3.astype(f32)
    part = unit // 2
    zero_part, one_part = (total[:part], total[part:])
    got = links.send(
        pick(core, one_part, zero_part),
        lambda x, y, z, c: (x, y, z, 1 - c) if z // 2 == c else None,
    )
    result = jnp.where(z // 2 == core, pick(core, zero_part, one_part), got)
    return result.T


def gather_vectors(links, vectors):
    lengths = [v.shape[0] for v in vectors]
    if not links.direct:
        return [lax.all_gather(v, "narrow", axis=0, tiled=True).astype(f32) for v in vectors]
    packed = jnp.concatenate(vectors)
    other = links.over_x(packed)
    full = []
    at = 0
    for length in lengths:
        mine, theirs = (packed[at : at + length], other[at : at + length])
        joined = jnp.concatenate([pick(links.x, mine, theirs), pick(links.x, theirs, mine)])
        full.append(joined.astype(f32))
        at += length
    return full


def vector_grads(links, sums):
    lengths = [v.shape[0] for v in sums]
    total = lax.psum(jnp.concatenate(sums), AXES)
    parts = []
    at = 0
    for length in lengths:
        own = length // links.count
        parts.append(lax.dynamic_slice_in_dim(total, at + links.x * own, own, 0))
        at += length
    return parts


def local(
    tokens,
    lengths,
    dropped,
    cotangent,
    first_gain,
    first_shift,
    qkv_weight,
    query_bias,
    value_bias,
    out_weight,
    out_bias,
    second_gain,
    second_shift,
    up_weight,
    up_bias,
    down_weight,
    down_bias,
):
    links = Links()
    rows, width = tokens.shape[1:]
    mask = key_mask(lengths[0], dropped[0], rows)
    inputs = tokens[0].astype(f32)
    grad_out = cotangent[0]
    gain1, shift1, q_bias, v_bias, o_bias, gain2, shift2, d_bias, u_bias = gather_vectors(
        links,
        [
            first_gain,
            first_shift,
            query_bias,
            value_bias,
            out_bias,
            second_gain,
            second_shift,
            down_bias,
            up_bias,
        ],
    )
    w_qkv = Weight(links, qkv_weight)
    w_out = Weight(links, out_weight)
    w_up = Weight(links, up_weight)
    w_down = Weight(links, down_weight)
    first = normed(inputs, gain1, shift1).astype(bf16)
    mixed = w_qkv.apply(first)
    query = (mixed[:, :width] + q_bias).astype(bf16)
    keys = mixed[:, width : 2 * width].astype(bf16)
    values = (mixed[:, 2 * width :] + v_bias).astype(bf16)
    attended, logsum = attention(query, keys, values, mask)
    middle = inputs + (w_out.apply(attended) + o_bias)
    second = normed(middle, gain2, shift2).astype(bf16)
    hidden = w_up.apply(second) + u_bias
    active = jax.nn.gelu(hidden, approximate=True).astype(bf16)
    g_down = weight_grad(links, active, grad_out)
    result = middle + (w_down.apply(active) + d_bias)
    output = result.astype(bf16)[None]
    d_active = w_down.apply_t(grad_out)
    unused, gelu_pull = jax.vjp(lambda v: jax.nn.gelu(v, approximate=True), hidden)
    d_hidden = gelu_pull(d_active)[0].astype(bf16)
    g_up = weight_grad(links, second, d_hidden)
    d_second = w_up.apply_t(d_hidden)
    unused, norm_pull = jax.vjp(normed, middle, gain2, shift2)
    d_middle, d_gain2, d_shift2 = norm_pull(d_second)
    d_middle = d_middle + grad_out.astype(f32)
    d_branch = d_middle.astype(bf16)
    g_out = weight_grad(links, attended, d_branch)
    d_attended = w_out.apply_t(d_branch).astype(bf16)
    d_query, d_keys, d_values = attention_back(query, keys, values, logsum, d_attended, mask)
    d_mixed = jnp.concatenate([d_query, d_keys, d_values], axis=1)
    g_qkv = weight_grad(links, first, d_mixed)
    d_first = w_qkv.apply_t(d_mixed)
    unused, first_pull = jax.vjp(normed, inputs, gain1, shift1)
    d_inputs, d_gain1, d_shift1 = first_pull(d_first)
    grad_tokens = (d_middle + d_inputs)[None]

    def column_sum(values):
        return jnp.sum(values.astype(f32), axis=0)

    v_gain1, v_shift1, v_q, v_v, v_o, v_gain2, v_shift2, v_up, v_down = vector_grads(
        links,
        [
            d_gain1,
            d_shift1,
            column_sum(d_query),
            column_sum(d_values),
            column_sum(d_branch),
            d_gain2,
            d_shift2,
            column_sum(d_hidden),
            column_sum(grad_out),
        ],
    )
    return (
        output,
        grad_tokens,
        v_gain1,
        v_shift1,
        g_qkv,
        v_q,
        v_v,
        g_out,
        v_o,
        v_gain2,
        v_shift2,
        g_up,
        v_up,
        g_down,
        v_down,
    )


def solution(mesh):
    batch = P(AXES, None, None)
    vector = P("narrow")
    matrix = P("narrow", None)
    return jax.shard_map(
        local,
        mesh=mesh,
        in_specs=(
            batch,
            P(AXES),
            P(AXES),
            batch,
            vector,
            vector,
            matrix,
            vector,
            vector,
            matrix,
            vector,
            vector,
            vector,
            matrix,
            vector,
            matrix,
            vector,
        ),
        out_specs=(
            batch,
            batch,
            vector,
            vector,
            P("narrow", "wide"),
            vector,
            vector,
            P("narrow", "wide"),
            vector,
            vector,
            vector,
            P("narrow", "wide"),
            vector,
            P("narrow", "wide"),
            vector,
        ),
        check_vma=False,
    )
```

profile of v0, /device:TPU:0, one launch (start us, length us, event | category | flops | bytes accessed | tf_op | source)
XLA Modules:
  0.0 569.3 jit_solution(4175647565305170686)
XLA Ops:
  4.1 2.5 constant_dynamic-slice_fusion.1
  6.6 3.0 collective-permute-start.9
  10.4 2.3 constant_dynamic-slice_fusion.3
  16.8 5.7 fusion.200
  22.5 2.5 constant_dynamic-slice_fusion
  30.9 35.9 %collective-permute-done = bf16[6720]{0:T(1024)(128)(2,1)S(1)} collective-permute-done((bf16[6720]{0:T(1024)(128)(2,1)S(1)}, bf16[6720]{0:T(1024)(128)(2,1)S(1)}, u32[]{:S(2)}, u32[]{:S(2)}) %collective-permute-start) | collective-permute-done | bytes 13472 | tf_op jit(solution)/shard_map/ppermute | solution.py:125
  67.5 4.1 fusion.169
  79.7 6.2 %collective-permute-done.6 = bf16[18,8,1120]{2,1,0:T(8,128)(2,1)S(1)} collective-permute-done((bf16[18,8,1120]{2,1,0:T(8,128)(2,1)}, bf16[18,8,1120]{2,1,0:T(8,128)(2,1)S(1)}, u32[]{:S(2)}, u32[]{:S(2)}) %collective-permute-start.6) | collective-permute-done | bytes 322592 | tf_op jit(solution)/shard_map/ppermute | solution.py:125
  89.5 14.6 %collective-permute-done.13 = bf16[70,8,1120]{2,1,0:T(8,128)(2,1)S(1)} collective-permute-done((bf16[70,8,1120]{2,1,0:T(8,128)(2,1)S(1)}, bf16[70,8,1120]{2,1,0:T(8,128)(2,1)S(1)}, u32[]{:S(2)}, u32[]{:S(2)}) %collective-permute-start.13) | collective-permute-done | bytes 1254432 | tf_op jit(solution)/shard_map/ppermute | solution.py:125
  108.6 2.6 collective-permute-done.2
  112.0 26.9 %collective-permute-done.14 = bf16[70,8,1120]{2,1,0:T(8,128)(2,1)} collective-permute-done((bf16[70,8,1120]{2,1,0:T(8,128)(2,1)S(1)}, bf16[70,8,1120]{2,1,0:T(8,128)(2,1)}, u32[]{:S(2)}, u32[]{:S(2)}) %collective-permute-start.14) | collective-permute-done | bytes 1254432 | tf_op jit(solution)/shard_map/ppermute | solution.py:125
  140.7 25.5 %collective-permute-done.10 = bf16[18,8,4480]{2,1,0:T(8,128)(2,1)} collective-permute-done((bf16[18,8,4480]{2,1,0:T(8,128)(2,1)}, bf16[18,8,4480]{2,1,0:T(8,128)(2,1)}, u32[]{:S(2)}, u32[]{:S(2)}) %collective-permute-start.10) | collective-permute-done | bytes 1290272 | tf_op jit(solution)/shard_map/ppermute | solution.py:125
  167.7 2.3 copy-done.24
  174.6 10.6 %while.28 = (s32[]{:T(128)}, bf16[4,256,5,56]{1,3,2,0:T(8,128)(2,1)}, f32[4,5,256,1]{2,1,3,0:T(8,128)S(1)}, bf16[4,256,5,56]{1,3,2,0:T(8,128)(2,1)}, bf16[4,256,...) while((s32[]{:T(128)}, ...), condition=%wide.region_5.6_spmd.clone, body=%wide.region_2.5_spmd.clone.sunk | while | flops 76354304 | bytes 4689241 | solution.py:65
  188.3 2.4 fusion.213
  191.8 2.7 constant_dynamic-update-slice_fusion.5
  194.5 2.0 fusion.163
  197.8 2.5 broadcast_select_fusion.18
  205.9 7.2 %convert_reduce_fusion = (f32[4480]{0:T(1024)S(1)}, bf16[256,4480]{1,0:T(8,128)(2,1)S(1)}, bf16[256,4480]{1,0:T(8,128)(2,1)}) fusion(f32[256,2240]{1,0:T(8,128)S(1)} %get-tuple-element.203, f32[256,2240]{1,0:T(8,128)S(1)} %get-tuple-element.202, f32[4480]{0:T(1024)S(1)} %copy-done.35, f32[256,4480]{1,0:T(8,128)S(1)} %fusion.163, ...), kind=kOutput, calls=%fused_computation.88 | convolution fusion | flops 1315610240 | bytes 19389440 | tf_op jit(solution)/shard_map/dot_general | solution.py:15
  225.7 22.3 %while.29 = (s32[]{:T(128)}, bf16[4,256,5,56]{1,3,2,0:T(8,128)(2,1)}, bf16[4,256,5,56]{1,3,2,0:T(8,128)(2,1)}, bf16[4,256,5,56]{1,3,2,0:T(8,128)(2,1)}, bf16[4,2...) while((s32[]{:T(128)}, ...), condition=%wide.region_12.13_spmd.clone, body=%wide.region_10.12_spmd.clone.sunk | while | flops 187069184 | bytes 13723021 | solution.py:88
  248.0 3.0 broadcast_select_fusion.6
  251.0 4.4 fusion.150
  255.8 6.7 %fusion.128 = f32[256,1120]{0,1:T(8,128)} fusion(bf16[2240,1120]{1,0:T(8,128)(2,1)} %param.40, pred[]{:T(512)S(6)} %eq.19, bf16[256,4480]{1,0:T(8,128)(2,1)} %get-tuple-element.206), kind=kOutput, calls=%fused_computation.196 | convolution fusion | flops 1285079040 | bytes 8667137 | tf_op jit(solution)/shard_map/dot_general | solution.py:15
  262.5 2.6 copy.63
  265.8 4.1 broadcast_select_fusion.33
  272.9 5.0 fusion.95
  280.9 40.1 %psum.7 = f32[13440]{0:T(1024)S(1)} all-reduce(f32[13440]{0:T(1024)S(1)} %concatenate.137), channel_id=1, replica_groups=mesh['wide'=16,'narrow'=2] {'wide','narrow'}, use_global_device_ids=true, to_apply=%region_24.25 | all-reduce | flops 13440 | bytes 107520 | tf_op jit(solution)/shard_map/psum | solution.py:265
  323.6 2.3 collective-permute-start.31
  328.9 4.7 collective-permute-done.31
  337.3 2.6 collective-permute-done.32
  340.2 2.6 collective-permute-done.30
  343.2 3.4 collective-permute-start.33
  361.8 2.4 copy.64
  364.2 2.7 fusion.151
  368.7 2.0 collective-permute-start.39
  371.5 11.1 %collective-permute-done.21 = bf16[2,420,560]{2,0,1:T(2,128)(2,1)} collective-permute-done((bf16[2,420,560]{2,0,1:T(2,128)(2,1)}, bf16[2,420,560]{2,0,1:T(2,128)(2,1)}, u32[]{:S(2)}, u32[]{:S(2)}) %collective-permute-start.21) | collective-permute-done | bytes 940832 | tf_op jit(solution)/shard_map/ppermute | solution.py:125
  382.6 3.3 fusion.209
  388.2 3.5 fusion.210
  395.5 29.3 %collective-permute-done.22 = bf16[420,560]{1,0:T(8,128)(2,1)S(1)} collective-permute-done((bf16[420,560]{1,0:T(8,128)(2,1)S(1)}, bf16[420,560]{1,0:T(8,128)(2,1)S(1)}, u32[]{:S(2)}, u32[]{:S(2)}) %collective-permute-start.22) | collective-permute-done | bytes 470432 | tf_op jit(solution)/shard_map/ppermute | solution.py:125
  425.9 2.5 collective-permute-start.23
  431.2 4.6 broadcast_select_fusion
  445.5 12.5 %collective-permute-done.24 = bf16[420,560]{1,0:T(8,128)(2,1)S(1)} collective-permute-done((bf16[420,560]{1,0:T(8,128)(2,1)S(1)}, bf16[420,560]{1,0:T(8,128)(2,1)S(1)}, u32[]{:S(2)}, u32[]{:S(2)}) %collective-permute-start.24) | collective-permute-done | bytes 470432 | tf_op jit(solution)/shard_map/ppermute | solution.py:125
  461.4 10.1 %collective-permute-done.51 = bf16[2,140,2240]{2,0,1:T(2,128)(2,1)S(1)} collective-permute-done((bf16[2,140,2240]{2,0,1:T(2,128)(2,1)S(1)}, bf16[2,140,2240]{2,0,1:T(2,128)(2,1)S(1)}, u32[]{:S(2)}, u32[]{:S(2)}) %collective-permute-start.51) | collective-permute-done | bytes 1254432 | tf_op jit(solution)/shard_map/ppermute | solution.py:125
  474.1 15.1 %collective-permute-done.49 = bf16[2,140,2240]{2,0,1:T(2,128)(2,1)S(1)} collective-permute-done((bf16[2,140,2240]{2,0,1:T(2,128)(2,1)S(1)}, bf16[2,140,2240]{2,0,1:T(2,128)(2,1)S(1)}, u32[]{:S(2)}, u32[]{:S(2)}) %collective-permute-start.49) | collective-permute-done | bytes 1254432 | tf_op jit(solution)/shard_map/ppermute | solution.py:125
  499.5 2.8 collective-permute-done.50
  504.3 9.6 %collective-permute-done.43 = bf16[560,560]{1,0:T(8,128)(2,1)S(1)} collective-permute-done((bf16[560,560]{1,0:T(8,128)(2,1)S(1)}, bf16[560,560]{1,0:T(8,128)(2,1)S(1)}, u32[]{:S(2)}, u32[]{:S(2)}) %collective-permute-start.43) | collective-permute-done | bytes 627232 | tf_op jit(solution)/shard_map/ppermute | solution.py:125
  515.8 16.9 %collective-permute-done.44 = bf16[560,560]{1,0:T(8,128)(2,1)S(1)} collective-permute-done((bf16[560,560]{1,0:T(8,128)(2,1)S(1)}, bf16[560,560]{1,0:T(8,128)(2,1)S(1)}, u32[]{:S(2)}, u32[]{:S(2)}) %collective-permute-start.44) | collective-permute-done | bytes 627232 | tf_op jit(solution)/shard_map/ppermute | solution.py:125
  537.2 26.2 %collective-permute-done.54 = bf16[140,2240]{1,0:T(8,128)(2,1)S(1)} collective-permute-done((bf16[140,2240]{1,0:T(8,128)(2,1)S(1)}, bf16[140,2240]{1,0:T(8,128)(2,1)S(1)}, u32[]{:S(2)}, u32[]{:S(2)}) %collective-permute-start.54) | collective-permute-done | bytes 627232 | tf_op jit(solution)/shard_map/ppermute | solution.py:125
  (412 shorter events, 170.3 us)
Async XLA Ops:
  6.6 99.9 %collective-permute-start.9 = (bf16[18,8,4480]{2,1,0:T(8,128)(2,1)}, bf16[18,8,4480]{2,1,0:T(8,128)(2,1)}, u32[]{:S(2)}, u32[]{:S(2)}) collective-permute-start(bf16[18,8,4480]{2,1,0:T(8,128)(2,1)} %constant_dynamic-slice_fusion.1), channel_id=1, source_target_pairs={{0,1},{1,0},{2,3},{3,2},{4,5},{5,4},{6,7},{7,6},{8,9},{9,8},{10,11... | collective-permute-start | bytes 3870728 | tf_op jit(solution)/shard_map/ppermute | solution.py:125
  10.4 65.4 %collective-permute-start.5 = (bf16[18,8,1120]{2,1,0:T(8,128)(2,1)}, bf16[18,8,1120]{2,1,0:T(8,128)(2,1)}, u32[]{:S(2)}, u32[]{:S(2)}) collective-permute-start(bf16[18,8,1120]{2,1,0:T(8,128)(2,1)} %constant_dynamic-slice_fusion.2), channel_id=1, source_target_pairs={{0,1},{1,0},{2,3},{3,2},{4,5},{5,4},{6,7},{7,6},{8,9},{9,8},{10,11... | collective-permute-start | bytes 967688 | tf_op jit(solution)/shard_map/ppermute | solution.py:125
  12.7 73.3 %collective-permute-start.1 = (bf16[18,8,3360]{2,1,0:T(8,128)(2,1)}, bf16[18,8,3360]{2,1,0:T(8,128)(2,1)}, u32[]{:S(2)}, u32[]{:S(2)}) collective-permute-start(bf16[18,8,3360]{2,1,0:T(8,128)(2,1)} %constant_dynamic-slice_fusion.3), channel_id=1, source_target_pairs={{0,1},{1,0},{2,3},{3,2},{4,5},{5,4},{6,7},{7,6},{8,9},{9,8},{10,11... | collective-permute-start | bytes 2903048 | tf_op jit(solution)/shard_map/ppermute | solution.py:125
  14.9 52.0 %collective-permute-start = (bf16[6720]{0:T(1024)(128)(2,1)S(1)}, bf16[6720]{0:T(1024)(128)(2,1)S(1)}, u32[]{:S(2)}, u32[]{:S(2)}) collective-permute-start(bf16[6720]{0:T(1024)(128)(2,1)S(1)} %concatenate.120), channel_id=1, source_target_pairs={{0,1},{1,0},{2,3},{3,2},{4,5},{5,4},{6,7},{7,6},{8,9},{9,8},{10,11... | collective-permute-start | bytes 40328 | tf_op jit(solution)/shard_map/ppermute | solution.py:125
  15.0 58.3 %collective-permute-start.47 = (bf16[256,560]{0,1:T(8,128)(2,1)S(1)}, bf16[256,560]{0,1:T(8,128)(2,1)S(1)}, u32[]{:S(2)}, u32[]{:S(2)}) collective-permute-start(bf16[256,560]{0,1:T(8,128)(2,1)S(1)} %get-tuple-element.251), channel_id=1, source_target_pairs={{0,2},{1,3},{2,0},{3,1},{4,6},{5,7},{6,4},{7,5},{8,10},{9,11},{10,... | collective-permute-start | bytes 860168 | tf_op jit(solution)/shard_map/ppermute | solution.py:125
  73.3 30.7 %collective-permute-start.13 = (bf16[70,8,1120]{2,1,0:T(8,128)(2,1)S(1)}, bf16[70,8,1120]{2,1,0:T(8,128)(2,1)S(1)}, u32[]{:S(2)}, u32[]{:S(2)}) collective-permute-start(bf16[70,8,1120]{2,1,0:T(8,128)(2,1)S(1)} %copy-done.30), channel_id=1, source_target_pairs={{0,1},{1,0},{2,3},{3,2},{4,5},{5,4},{6,7},{7,6},{8,9},{9,8},{10,11... | collective-permute-start | bytes 3763208 | tf_op jit(solution)/shard_map/ppermute | solution.py:125
  75.8 10.1 %collective-permute-start.6 = (bf16[18,8,1120]{2,1,0:T(8,128)(2,1)}, bf16[18,8,1120]{2,1,0:T(8,128)(2,1)S(1)}, u32[]{:S(2)}, u32[]{:S(2)}) collective-permute-start(bf16[18,8,1120]{2,1,0:T(8,128)(2,1)} %collective-permute-done.5), channel_id=1, source_target_pairs={{0,4},{1,5},{2,6},{3,7},{4,0},{5,1},{6,2},{7,3},{8,12},{9,13},{10,... | collective-permute-start | bytes 967688 | tf_op jit(solution)/shard_map/ppermute | solution.py:125
  86.0 25.2 %collective-permute-start.2 = (bf16[18,8,3360]{2,1,0:T(8,128)(2,1)}, bf16[18,8,3360]{2,1,0:T(8,128)(2,1)S(1)}, u32[]{:S(2)}, u32[]{:S(2)}) collective-permute-start(bf16[18,8,3360]{2,1,0:T(8,128)(2,1)} %collective-permute-done.1), channel_id=1, source_target_pairs={{0,4},{1,5},{2,6},{3,7},{4,0},{5,1},{6,2},{7,3},{8,12},{9,13},{10,... | collective-permute-start | bytes 2903048 | tf_op jit(solution)/shard_map/ppermute | solution.py:125
  87.6 23.7 %collective-permute-start.3 = (bf16[18,8,3360]{2,1,0:T(8,128)(2,1)}, bf16[18,8,3360]{2,1,0:T(8,128)(2,1)S(1)}, u32[]{:S(2)}, u32[]{:S(2)}) collective-permute-start(bf16[18,8,3360]{2,1,0:T(8,128)(2,1)} %collective-permute-done.1), channel_id=1, source_target_pairs={{0,2},{1,3},{2,0},{3,1},{4,6},{5,7},{6,4},{7,5},{8,10},{9,11},{10,... | collective-permute-start | bytes 2903048 | tf_op jit(solution)/shard_map/ppermute | solution.py:125
  104.1 34.9 %collective-permute-start.14 = (bf16[70,8,1120]{2,1,0:T(8,128)(2,1)S(1)}, bf16[70,8,1120]{2,1,0:T(8,128)(2,1)}, u32[]{:S(2)}, u32[]{:S(2)}) collective-permute-start(bf16[70,8,1120]{2,1,0:T(8,128)(2,1)S(1)} %collective-permute-done.13), channel_id=1, source_target_pairs={{0,4},{1,5},{2,6},{3,7},{4,0},{5,1},{6,2},{7,3},{8,12},{9,13},{10,... | collective-permute-start | bytes 3763208 | tf_op jit(solution)/shard_map/ppermute | solution.py:125
  105.9 34.6 %collective-permute-start.15 = (bf16[70,8,1120]{2,1,0:T(8,128)(2,1)S(1)}, bf16[70,8,1120]{2,1,0:T(8,128)(2,1)S(1)}, u32[]{:S(2)}, u32[]{:S(2)}) collective-permute-start(bf16[70,8,1120]{2,1,0:T(8,128)(2,1)S(1)} %collective-permute-done.13), channel_id=1, source_target_pairs={{0,2},{1,3},{2,0},{3,1},{4,6},{5,7},{6,4},{7,5},{8,10},{9,11},{10,... | collective-permute-start | bytes 3763208 | tf_op jit(solution)/shard_map/ppermute | solution.py:125
  106.4 59.7 %collective-permute-start.10 = (bf16[18,8,4480]{2,1,0:T(8,128)(2,1)}, bf16[18,8,4480]{2,1,0:T(8,128)(2,1)}, u32[]{:S(2)}, u32[]{:S(2)}) collective-permute-start(bf16[18,8,4480]{2,1,0:T(8,128)(2,1)} %collective-permute-done.9), channel_id=1, source_target_pairs={{0,4},{1,5},{2,6},{3,7},{4,0},{5,1},{6,2},{7,3},{8,12},{9,13},{10,... | collective-permute-start | bytes 3870728 | tf_op jit(solution)/shard_map/ppermute | solution.py:125
  111.2 80.6 %collective-permute-start.11 = (bf16[18,8,4480]{2,1,0:T(8,128)(2,1)}, bf16[18,8,4480]{2,1,0:T(8,128)(2,1)}, u32[]{:S(2)}, u32[]{:S(2)}) collective-permute-start(bf16[18,8,4480]{2,1,0:T(8,128)(2,1)} %collective-permute-done.9), channel_id=1, source_target_pairs={{0,2},{1,3},{2,0},{3,1},{4,6},{5,7},{6,4},{7,5},{8,10},{9,11},{10,... | collective-permute-start | bytes 3870728 | tf_op jit(solution)/shard_map/ppermute | solution.py:125
  111.3 56.3 %collective-permute-start.4 = (bf16[18,8,3360]{2,1,0:T(8,128)(2,1)S(1)}, bf16[18,8,3360]{2,1,0:T(8,128)(2,1)S(1)}, u32[]{:S(2)}, u32[]{:S(2)}) collective-permute-start(bf16[18,8,3360]{2,1,0:T(8,128)(2,1)S(1)} %collective-permute-done.2), channel_id=1, source_target_pairs={{0,2},{1,3},{2,0},{3,1},{4,6},{5,7},{6,4},{7,5},{8,10},{9,11},{10,... | collective-permute-start | bytes 2903048 | tf_op jit(solution)/shard_map/ppermute | solution.py:125
  139.0 61.4 %collective-permute-start.16 = (bf16[70,8,1120]{2,1,0:T(8,128)(2,1)}, bf16[70,8,1120]{2,1,0:T(8,128)(2,1)}, u32[]{:S(2)}, u32[]{:S(2)}) collective-permute-start(bf16[70,8,1120]{2,1,0:T(8,128)(2,1)} %collective-permute-done.14), channel_id=1, source_target_pairs={{0,2},{1,3},{2,0},{3,1},{4,6},{5,7},{6,4},{7,5},{8,10},{9,11},{10,... | collective-permute-start | bytes 3763208 | tf_op jit(solution)/shard_map/ppermute | solution.py:125
  166.2 38.2 %collective-permute-start.12 = (bf16[18,8,4480]{2,1,0:T(8,128)(2,1)}, bf16[18,8,4480]{2,1,0:T(8,128)(2,1)}, u32[]{:S(2)}, u32[]{:S(2)}) collective-permute-start(bf16[18,8,4480]{2,1,0:T(8,128)(2,1)} %collective-permute-done.10), channel_id=1, source_target_pairs={{0,2},{1,3},{2,0},{3,1},{4,6},{5,7},{6,4},{7,5},{8,10},{9,11},{10,... | collective-permute-start | bytes 3870728 | tf_op jit(solution)/shard_map/ppermute | solution.py:125
  255.4 174.3 %collective-permute-start.48 = (bf16[256,4480]{1,0:T(8,128)(2,1)}, bf16[256,4480]{1,0:T(8,128)(2,1)}, u32[]{:S(2)}, u32[]{:S(2)}) collective-permute-start(bf16[256,4480]{1,0:T(8,128)(2,1)} %get-tuple-element.206), channel_id=1, source_target_pairs={{0,2},{1,3},{2,0},{3,1},{4,6},{5,7},{6,4},{7,5},{8,10},{9,11},{10,... | collective-permute-start | bytes 6881288 | tf_op jit(solution)/shard_map/ppermute | solution.py:125
  265.2 96.6 %collective-permute-start.37 = (bf16[256,2240]{0,1:T(8,128)(2,1)}, bf16[256,2240]{0,1:T(8,128)(2,1)}, u32[]{:S(2)}, u32[]{:S(2)}) collective-permute-start(bf16[256,2240]{0,1:T(8,128)(2,1)} %copy.63), channel_id=1, source_target_pairs={{0,2},{1,3},{2,0},{3,1},{4,6},{5,7},{6,4},{7,5},{8,10},{9,11},{10,... | collective-permute-start | bytes 3440648 | tf_op jit(solution)/shard_map/ppermute | solution.py:125
  265.3 56.4 %collective-permute-start.27 = (bf16[256,560]{0,1:T(8,128)(2,1)}, bf16[256,560]{0,1:T(8,128)(2,1)}, u32[]{:S(2)}, u32[]{:S(2)}) collective-permute-start(bf16[256,560]{0,1:T(8,128)(2,1)} %get-tuple-element.257), channel_id=1, source_target_pairs={{0,2},{1,3},{2,0},{3,1},{4,6},{5,7},{6,4},{7,5},{8,10},{9,11},{10,... | collective-permute-start | bytes 860168 | tf_op jit(solution)/shard_map/ppermute | solution.py:125
  265.8 82.2 %collective-permute-start.17 = (bf16[256,1680]{0,1:T(8,128)(2,1)}, bf16[256,1680]{0,1:T(8,128)(2,1)}, u32[]{:S(2)}, u32[]{:S(2)}) collective-permute-start(bf16[256,1680]{0,1:T(8,128)(2,1)} %get-tuple-element.225), channel_id=1, source_target_pairs={{0,2},{1,3},{2,0},{3,1},{4,6},{5,7},{6,4},{7,5},{8,10},{9,11},{10,... | collective-permute-start | bytes 2580488 | tf_op jit(solution)/shard_map/ppermute | solution.py:125
  326.7 10.1 %collective-permute-start.29 = (bf16[2,140,560]{2,1,0:T(8,128)(2,1)S(1)}, bf16[2,140,560]{2,1,0:T(8,128)(2,1)S(1)}, u32[]{:S(2)}, u32[]{:S(2)}) collective-permute-start(bf16[2,140,560]{2,1,0:T(8,128)(2,1)S(1)} %pad_maximum_fusion.20), channel_id=1, source_target_pairs={{0,1},{1,0},{2,3},{3,2},{4,5},{5,4},{6,7},{7,6},{8,9},{9,8},{10,11... | collective-permute-start | bytes 940808 | tf_op jit(solution)/shard_map/ppermute | solution.py:125
  343.2 14.8 %collective-permute-start.33 = (bf16[140,560]{1,0:T(8,128)(2,1)S(1)}, bf16[140,560]{1,0:T(8,128)(2,1)S(1)}, u32[]{:S(2)}, u32[]{:S(2)}) collective-permute-start(bf16[140,560]{1,0:T(8,128)(2,1)S(1)} %get-tuple-element.246), channel_id=1, source_target_pairs={{0,8},{1,9},{4,12},{5,13},{8,0},{9,1},{12,4},{13,5},{18,26},{19,27... | collective-permute-start | bytes 470408 | tf_op jit(solution)/shard_map/ppermute | solution.py:125
  346.6 13.7 %collective-permute-start.35 = (bf16[140,560]{1,0:T(8,128)(2,1)S(1)}, bf16[140,560]{1,0:T(8,128)(2,1)S(1)}, u32[]{:S(2)}, u32[]{:S(2)}) collective-permute-start(bf16[140,560]{1,0:T(8,128)(2,1)S(1)} %get-tuple-element.246), channel_id=1, source_target_pairs={{2,26},{3,27},{6,30},{7,31},{10,18},{11,19},{14,22},{15,23},{16,8}... | collective-permute-start | bytes 470408 | tf_op jit(solution)/shard_map/ppermute | solution.py:125
  347.9 12.0 %collective-permute-start.34 = (bf16[140,560]{1,0:T(8,128)(2,1)S(1)}, bf16[140,560]{1,0:T(8,128)(2,1)S(1)}, u32[]{:S(2)}, u32[]{:S(2)}) collective-permute-start(bf16[140,560]{1,0:T(8,128)(2,1)S(1)} %get-tuple-element.245), channel_id=1, source_target_pairs={{2,18},{3,19},{6,22},{7,23},{10,26},{11,27},{14,30},{15,31},{16,0}... | collective-permute-start | bytes 470408 | tf_op jit(solution)/shard_map/ppermute | solution.py:125
  358.0 30.3 %collective-permute-start.19 = (bf16[2,420,560]{2,0,1:T(2,128)(2,1)}, bf16[2,420,560]{2,0,1:T(2,128)(2,1)}, u32[]{:S(2)}, u32[]{:S(2)}) collective-permute-start(bf16[2,420,560]{2,0,1:T(2,128)(2,1)} %copy.57), channel_id=1, source_target_pairs={{0,1},{1,0},{2,3},{3,2},{4,5},{5,4},{6,7},{7,6},{8,9},{9,8},{10,11... | collective-permute-start | bytes 2822408 | tf_op jit(solution)/shard_map/ppermute | solution.py:125
  359.9 22.7 %collective-permute-start.21 = (bf16[2,420,560]{2,0,1:T(2,128)(2,1)}, bf16[2,420,560]{2,0,1:T(2,128)(2,1)}, u32[]{:S(2)}, u32[]{:S(2)}) collective-permute-start(bf16[2,420,560]{2,0,1:T(2,128)(2,1)} %copy.60), channel_id=1, source_target_pairs={{0,4},{1,5},{2,6},{3,7},{4,0},{5,1},{6,2},{7,3},{8,12},{9,13},{10,... | collective-permute-start | bytes 2822408 | tf_op jit(solution)/shard_map/ppermute | solution.py:125
  368.7 72.9 %collective-permute-start.39 = (bf16[2,560,560]{2,1,0:T(8,128)(2,1)S(1)}, bf16[2,560,560]{2,1,0:T(8,128)(2,1)S(1)}, u32[]{:S(2)}, u32[]{:S(2)}) collective-permute-start(bf16[2,560,560]{2,1,0:T(8,128)(2,1)S(1)} %pad_maximum_fusion.3), channel_id=1, source_target_pairs={{0,1},{1,0},{2,3},{3,2},{4,5},{5,4},{6,7},{7,6},{8,9},{9,8},{10,11... | collective-permute-start | bytes 3763208 | tf_op jit(solution)/shard_map/ppermute | solution.py:125
  386.5 38.3 %collective-permute-start.22 = (bf16[420,560]{1,0:T(8,128)(2,1)S(1)}, bf16[420,560]{1,0:T(8,128)(2,1)S(1)}, u32[]{:S(2)}, u32[]{:S(2)}) collective-permute-start(bf16[420,560]{1,0:T(8,128)(2,1)S(1)} %fusion.111), channel_id=1, source_target_pairs={{0,1},{1,0},{2,3},{3,2},{4,5},{5,4},{6,7},{7,6},{8,9},{9,8},{10,11... | collective-permute-start | bytes 1411208 | tf_op jit(solution)/shard_map/ppermute | solution.py:125
  392.3 33.0 %collective-permute-start.20 = (bf16[420,560]{1,0:T(8,128)(2,1)S(1)}, bf16[420,560]{1,0:T(8,128)(2,1)S(1)}, u32[]{:S(2)}, u32[]{:S(2)}) collective-permute-start(bf16[420,560]{1,0:T(8,128)(2,1)S(1)} %fusion.110), channel_id=1, source_target_pairs={{0,4},{1,5},{2,6},{3,7},{4,0},{5,1},{6,2},{7,3},{8,12},{9,13},{10,... | collective-permute-start | bytes 1411208 | tf_op jit(solution)/shard_map/ppermute | solution.py:125
  394.0 46.2 %collective-permute-start.41 = (bf16[2,560,560]{2,1,0:T(8,128)(2,1)S(1)}, bf16[2,560,560]{2,1,0:T(8,128)(2,1)S(1)}, u32[]{:S(2)}, u32[]{:S(2)}) collective-permute-start(bf16[2,560,560]{2,1,0:T(8,128)(2,1)S(1)} %pad_maximum_fusion.4), channel_id=1, source_target_pairs={{0,4},{1,5},{2,6},{3,7},{4,0},{5,1},{6,2},{7,3},{8,12},{9,13},{10,... | collective-permute-start | bytes 3763208 | tf_op jit(solution)/shard_map/ppermute | solution.py:125
  425.9 18.0 %collective-permute-start.23 = (bf16[420,560]{1,0:T(8,128)(2,1)S(1)}, bf16[420,560]{1,0:T(8,128)(2,1)S(1)}, u32[]{:S(2)}, u32[]{:S(2)}) collective-permute-start(bf16[420,560]{1,0:T(8,128)(2,1)S(1)} %get-tuple-element.220), channel_id=1, source_target_pairs={{0,8},{1,9},{4,12},{5,13},{8,0},{9,1},{12,4},{13,5},{18,26},{19,27... | collective-permute-start | bytes 1411208 | tf_op jit(solution)/shard_map/ppermute | solution.py:125
  428.4 29.9 %collective-permute-start.25 = (bf16[420,560]{1,0:T(8,128)(2,1)S(1)}, bf16[420,560]{1,0:T(8,128)(2,1)S(1)}, u32[]{:S(2)}, u32[]{:S(2)}) collective-permute-start(bf16[420,560]{1,0:T(8,128)(2,1)S(1)} %get-tuple-element.220), channel_id=1, source_target_pairs={{2,26},{3,27},{6,30},{7,31},{10,18},{11,19},{14,22},{15,23},{16,8}... | collective-permute-start | bytes 1411208 | tf_op jit(solution)/shard_map/ppermute | solution.py:125
  429.7 28.3 %collective-permute-start.24 = (bf16[420,560]{1,0:T(8,128)(2,1)S(1)}, bf16[420,560]{1,0:T(8,128)(2,1)S(1)}, u32[]{:S(2)}, u32[]{:S(2)}) collective-permute-start(bf16[420,560]{1,0:T(8,128)(2,1)S(1)} %get-tuple-element.219), channel_id=1, source_target_pairs={{2,18},{3,19},{6,22},{7,23},{10,26},{11,27},{14,30},{15,31},{16,0}... | collective-permute-start | bytes 1411208 | tf_op jit(solution)/shard_map/ppermute | solution.py:125
  440.2 31.3 %collective-permute-start.51 = (bf16[2,140,2240]{2,0,1:T(2,128)(2,1)S(1)}, bf16[2,140,2240]{2,0,1:T(2,128)(2,1)S(1)}, u32[]{:S(2)}, u32[]{:S(2)}) collective-permute-start(bf16[2,140,2240]{2,0,1:T(2,128)(2,1)S(1)} %copy.68), channel_id=1, source_target_pairs={{0,4},{1,5},{2,6},{3,7},{4,0},{5,1},{6,2},{7,3},{8,12},{9,13},{10,... | collective-permute-start | bytes 3763208 | tf_op jit(solution)/shard_map/ppermute | solution.py:125
  441.6 19.0 %collective-permute-start.42 = (bf16[560,560]{1,0:T(8,128)(2,1)S(1)}, bf16[560,560]{1,0:T(8,128)(2,1)S(1)}, u32[]{:S(2)}, u32[]{:S(2)}) collective-permute-start(bf16[560,560]{1,0:T(8,128)(2,1)S(1)} %fusion.109), channel_id=1, source_target_pairs={{0,1},{1,0},{2,3},{3,2},{4,5},{5,4},{6,7},{7,6},{8,9},{9,8},{10,11... | collective-permute-start | bytes 1881608 | tf_op jit(solution)/shard_map/ppermute | solution.py:125
  444.0 121.4 %collective-permute-start.36 = (f32[70,560]{1,0:T(8,128)S(1)}, f32[70,560]{1,0:T(8,128)S(1)}, u32[]{:S(2)}, u32[]{:S(2)}) collective-permute-start(f32[70,560]{1,0:T(8,128)S(1)} %copy-done.33), channel_id=1, source_target_pairs={{0,2},{1,3},{4,6},{5,7},{8,10},{9,11},{12,14},{13,15},{18,16},{19,... | collective-permute-start | bytes 470408 | tf_op jit(solution)/shard_map/ppermute | solution.py:125
  458.0 31.2 %collective-permute-start.49 = (bf16[2,140,2240]{2,0,1:T(2,128)(2,1)S(1)}, bf16[2,140,2240]{2,0,1:T(2,128)(2,1)S(1)}, u32[]{:S(2)}, u32[]{:S(2)}) collective-permute-start(bf16[2,140,2240]{2,0,1:T(2,128)(2,1)S(1)} %copy.65), channel_id=1, source_target_pairs={{0,1},{1,0},{2,3},{3,2},{4,5},{5,4},{6,7},{7,6},{8,9},{9,8},{10,11... | collective-permute-start | bytes 3763208 | tf_op jit(solution)/shard_map/ppermute | solution.py:125
  458.3 33.9 %collective-permute-start.40 = (bf16[560,560]{1,0:T(8,128)(2,1)S(1)}, bf16[560,560]{1,0:T(8,128)(2,1)S(1)}, u32[]{:S(2)}, u32[]{:S(2)}) collective-permute-start(bf16[560,560]{1,0:T(8,128)(2,1)S(1)} %fusion.108), channel_id=1, source_target_pairs={{0,4},{1,5},{2,6},{3,7},{4,0},{5,1},{6,2},{7,3},{8,12},{9,13},{10,... | collective-permute-start | bytes 1881608 | tf_op jit(solution)/shard_map/ppermute | solution.py:125
  473.8 23.9 %collective-permute-start.52 = (bf16[140,2240]{1,0:T(8,128)(2,1)S(1)}, bf16[140,2240]{1,0:T(8,128)(2,1)S(1)}, u32[]{:S(2)}, u32[]{:S(2)}) collective-permute-start(bf16[140,2240]{1,0:T(8,128)(2,1)S(1)} %fusion.76), channel_id=1, source_target_pairs={{0,1},{1,0},{2,3},{3,2},{4,5},{5,4},{6,7},{7,6},{8,9},{9,8},{10,11... | collective-permute-start | bytes 1881608 | tf_op jit(solution)/shard_map/ppermute | solution.py:125
  491.6 10.7 %collective-permute-start.50 = (bf16[140,2240]{1,0:T(8,128)(2,1)S(1)}, bf16[140,2240]{1,0:T(8,128)(2,1)S(1)}, u32[]{:S(2)}, u32[]{:S(2)}) collective-permute-start(bf16[140,2240]{1,0:T(8,128)(2,1)S(1)} %fusion.75), channel_id=1, source_target_pairs={{0,4},{1,5},{2,6},{3,7},{4,0},{5,1},{6,2},{7,3},{8,12},{9,13},{10,... | collective-permute-start | bytes 1881608 | tf_op jit(solution)/shard_map/ppermute | solution.py:125
  493.1 20.8 %collective-permute-start.43 = (bf16[560,560]{1,0:T(8,128)(2,1)S(1)}, bf16[560,560]{1,0:T(8,128)(2,1)S(1)}, u32[]{:S(2)}, u32[]{:S(2)}) collective-permute-start(bf16[560,560]{1,0:T(8,128)(2,1)S(1)} %get-tuple-element.210), channel_id=1, source_target_pairs={{0,8},{1,9},{4,12},{5,13},{8,0},{9,1},{12,4},{13,5},{18,26},{19,27... | collective-permute-start | bytes 1881608 | tf_op jit(solution)/shard_map/ppermute | solution.py:125
  495.0 39.0 %collective-permute-start.45 = (bf16[560,560]{1,0:T(8,128)(2,1)S(1)}, bf16[560,560]{1,0:T(8,128)(2,1)S(1)}, u32[]{:S(2)}, u32[]{:S(2)}) collective-permute-start(bf16[560,560]{1,0:T(8,128)(2,1)S(1)} %get-tuple-element.210), channel_id=1, source_target_pairs={{2,26},{3,27},{6,30},{7,31},{10,18},{11,19},{14,22},{15,23},{16,8}... | collective-permute-start | bytes 1881608 | tf_op jit(solution)/shard_map/ppermute | solution.py:125
  497.6 35.1 %collective-permute-start.44 = (bf16[560,560]{1,0:T(8,128)(2,1)S(1)}, bf16[560,560]{1,0:T(8,128)(2,1)S(1)}, u32[]{:S(2)}, u32[]{:S(2)}) collective-permute-start(bf16[560,560]{1,0:T(8,128)(2,1)S(1)} %get-tuple-element.209), channel_id=1, source_target_pairs={{2,18},{3,19},{6,22},{7,23},{10,26},{11,27},{14,30},{15,31},{16,0}... | collective-permute-start | bytes 1881608 | tf_op jit(solution)/shard_map/ppermute | solution.py:125
  502.3 63.8 %collective-permute-start.26 = (f32[210,560]{1,0:T(8,128)S(1)}, f32[210,560]{1,0:T(8,128)S(1)}, u32[]{:S(2)}, u32[]{:S(2)}) collective-permute-start(f32[210,560]{1,0:T(8,128)S(1)} %slice_select_fusion.2), channel_id=1, source_target_pairs={{0,2},{1,3},{4,6},{5,7},{8,10},{9,11},{12,14},{13,15},{18,16},{19,... | collective-permute-start | bytes 1411208 | tf_op jit(solution)/shard_map/ppermute | solution.py:125
  513.9 22.0 %collective-permute-start.53 = (bf16[140,2240]{1,0:T(8,128)(2,1)S(1)}, bf16[140,2240]{1,0:T(8,128)(2,1)S(1)}, u32[]{:S(2)}, u32[]{:S(2)}) collective-permute-start(bf16[140,2240]{1,0:T(8,128)(2,1)S(1)} %get-tuple-element.212), channel_id=1, source_target_pairs={{0,8},{1,9},{4,12},{5,13},{8,0},{9,1},{12,4},{13,5},{18,26},{19,27... | collective-permute-start | bytes 1881608 | tf_op jit(solution)/shard_map/ppermute | solution.py:125
  532.7 30.7 %collective-permute-start.55 = (bf16[140,2240]{1,0:T(8,128)(2,1)S(1)}, bf16[140,2240]{1,0:T(8,128)(2,1)S(1)}, u32[]{:S(2)}, u32[]{:S(2)}) collective-permute-start(bf16[140,2240]{1,0:T(8,128)(2,1)S(1)} %get-tuple-element.212), channel_id=1, source_target_pairs={{2,26},{3,27},{6,30},{7,31},{10,18},{11,19},{14,22},{15,23},{16,8}... | collective-permute-start | bytes 1881608 | tf_op jit(solution)/shard_map/ppermute | solution.py:125
  534.0 29.4 %collective-permute-start.54 = (bf16[140,2240]{1,0:T(8,128)(2,1)S(1)}, bf16[140,2240]{1,0:T(8,128)(2,1)S(1)}, u32[]{:S(2)}, u32[]{:S(2)}) collective-permute-start(bf16[140,2240]{1,0:T(8,128)(2,1)S(1)} %get-tuple-element.211), channel_id=1, source_target_pairs={{2,18},{3,19},{6,22},{7,23},{10,26},{11,27},{14,30},{15,31},{16,0}... | collective-permute-start | bytes 1881608 | tf_op jit(solution)/shard_map/ppermute | solution.py:125
  535.9 31.2 %collective-permute-start.46 = (f32[280,560]{1,0:T(8,128)S(1)}, f32[280,560]{1,0:T(8,128)S(1)}, u32[]{:S(2)}, u32[]{:S(2)}) collective-permute-start(f32[280,560]{1,0:T(8,128)S(1)} %slice_select_fusion), channel_id=1, source_target_pairs={{0,2},{1,3},{4,6},{5,7},{8,10},{9,11},{12,14},{13,15},{18,16},{19,... | collective-permute-start | bytes 1881608 | tf_op jit(solution)/shard_map/ppermute | solution.py:125
  (72 other events, 485.0 us)
where the time goes:
time: 580 us; the launch traced here: 569 us
  waiting for transfers between devices  260 us (45%)
  matrix products  97.7 us (17%)
  local copies, waits for them, and re-layouts  58.4 us (10%)
  starting transfers between devices  58.3 us (10%)
  other arithmetic  43.3 us (7%)
  blocking collectives  40.1 us (7%)
  between operations  11.6 us (2%)
    ppermute x57, waiting for transfers between devices, send(): return lax.ppermute(value, AXES, self.table(move))  260 us
    ppermute x57, starting transfers between devices, send(): return lax.ppermute(value, AXES, self.table(move))  58.3 us
    psum x1, blocking collectives, vector_grads(): total = lax.psum(jnp.concatenate(sums), AXES)  40.1 us
    dot_general x8, matrix products, dot(): return jnp.dot(left, right, preferred_element_type=f32)  31.4 us
    dot_general x8, matrix products, dot_t(): lax.dot_general(left, right, (((1,), (1,)), ((), ())), preferred_element_...  20.1 us
    dot_general x32, matrix products, tdot(): lax.dot_general(left, right, (((0,), (0,)), ((), ())), preferred_element_...  17.9 us
    select_n x15, other arithmetic, pick(): return jnp.where(which == 0, zero, one)  16.4 us
    dynamic_update_slice x16, local copies, waits for them, and re-layouts, gather_other(): whole = lax.dynamic_update_slice_in_dim(whole, value, spot, 0)  13.5 us
  transfers between devices with their start and end apart: 57, of which 22 were waited for; matrix products, arithmetic and copies ran while one was open for 24% of the time, Pallas kernels for 0%

commit v1 on v0

--- a/solution.py
+++ b/solution.py
@@ -2,6 +2,7 @@
 import jax.numpy as jnp
 from jax import lax
 from jax.sharding import PartitionSpec as P
+from jax.lax import all_gather
 
 HEAD = 56
 epsilon = 1e-05
@@ -262,7 +263,7 @@
 
 def vector_grads(links, sums):
     lengths = [v.shape[0] for v in sums]
-    total = lax.psum(jnp.concatenate(sums), AXES)
+    total = jnp.sum(all_gather(jnp.concatenate(sums), AXES), axis=0)
     parts = []
     at = 0
     for length in lengths:

time: 580 us -> 565 us (0.974)
  blocking collectives: 40.1 us -> 0 us
  between operations: 11.6 us -> 25 us
  matrix products: 97.7 us -> 111 us
  waiting for transfers between devices: 260 us -> 252 us
    psum x1 -> x0, blocking collectives: 40.1 us -> none  [vector_grads(): total = lax.psum(jnp.concatenate(sums), AXES)]
    ppermute x57, waiting for transfers between devices: 260 us -> 252 us  [send(): return lax.ppermute(value, AXES, self.table(move))]
    dot_general x8, matrix products: 3.7 us -> 11 us  [scores_of(): jnp.einsum('qhe,khe->hqk', query, keys, preferred_element_type=f32)]
  transfers between devices with their start and end apart: 57 -> 58, of which waited for: 22 -> 21; matrix products, arithmetic and copies ran while one was open for 24% -> 25% of each run, Pallas kernels for 0% -> 0%
where the time goes in v1:
time: 565 us; the launch traced here: 554 us
  waiting for transfers between devices  252 us (45%)
  matrix products  111 us (20%)
  starting transfers between devices  63.7 us (11%)
  local copies, waits for them, and re-layouts  55.3 us (10%)
  other arithmetic  46.5 us (8%)
  between operations  25 us (4%)
    ppermute x57, waiting for transfers between devices, send(): return lax.ppermute(value, AXES, self.table(move))  252 us
    ppermute x57, starting transfers between devices, send(): return lax.ppermute(value, AXES, self.table(move))  63.7 us
    dot_general x8, matrix products, dot(): return jnp.dot(left, right, preferred_element_type=f32)  33.5 us
    dot_general x8, matrix products, dot_t(): lax.dot_general(left, right, (((1,), (1,)), ((), ())), preferred_element_...  19.4 us
    dot_general x32, matrix products, tdot(): lax.dot_general(left, right, (((0,), (0,)), ((), ())), preferred_element_...  18 us
    select_n x15, other arithmetic, pick(): return jnp.where(which == 0, zero, one)  16.5 us
    dynamic_update_slice x16, local copies, waits for them, and re-layouts, gather_other(): whole = lax.dynamic_update_slice_in_dim(whole, value, spot, 0)  13.5 us
  transfers between devices with their start and end apart: 58, of which 21 were waited for; matrix products, arithmetic and copies ran while one was open for 25% of the time, Pallas kernels for 0%

profile of v1, /device:TPU:0, one launch (start us, length us, event | category | flops | bytes accessed | tf_op | source)
XLA Modules:
  0.0 554.5 jit_solution(11278502881666388234)
XLA Ops:
  10.7 2.5 constant_dynamic-slice_fusion.1
  13.2 3.0 collective-permute-start.9
  17.0 2.3 constant_dynamic-slice_fusion.3
  19.3 2.0 collective-permute-start.1
  24.1 5.7 %fusion.200 = f32[256,2240]{1,0:T(8,128)} fusion(bf16[2240,1120]{1,0:T(8,128)(2,1)} %param.40, bf16[1,256,1120]{1,2,0:T(8,128)(2,1)S(1)} %copy-done.14), kind=kOutput, calls=%fused_computation.445 | convolution fusion | flops 1284505600 | bytes 7884800 | tf_op jit(solution)/shard_map/dot_general | solution.py:24
  37.2 36.3 %collective-permute-done = bf16[6720]{0:T(1024)(128)(2,1)S(1)} collective-permute-done((bf16[6720]{0:T(1024)(128)(2,1)S(1)}, bf16[6720]{0:T(1024)(128)(2,1)S(1)}, u32[]{:S(2)}, u32[]{:S(2)}) %collective-permute-start) | collective-permute-done | bytes 13472 | tf_op jit(solution)/shard_map/ppermute | solution.py:126
  74.8 4.1 fusion.169
  87.6 6.1 %collective-permute-done.6 = bf16[18,8,1120]{2,1,0:T(8,128)(2,1)S(1)} collective-permute-done((bf16[18,8,1120]{2,1,0:T(8,128)(2,1)}, bf16[18,8,1120]{2,1,0:T(8,128)(2,1)S(1)}, u32[]{:S(2)}, u32[]{:S(2)}) %collective-permute-start.6) | collective-permute-done | bytes 322592 | tf_op jit(solution)/shard_map/ppermute | solution.py:126
  97.3 13.5 %collective-permute-done.13 = bf16[70,8,1120]{2,1,0:T(8,128)(2,1)S(1)} collective-permute-done((bf16[70,8,1120]{2,1,0:T(8,128)(2,1)S(1)}, bf16[70,8,1120]{2,1,0:T(8,128)(2,1)S(1)}, u32[]{:S(2)}, u32[]{:S(2)}) %collective-permute-start.13) | collective-permute-done | bytes 1254432 | tf_op jit(solution)/shard_map/ppermute | solution.py:126
  115.3 3.7 collective-permute-done.2
  119.8 26.9 %collective-permute-done.14 = bf16[70,8,1120]{2,1,0:T(8,128)(2,1)} collective-permute-done((bf16[70,8,1120]{2,1,0:T(8,128)(2,1)S(1)}, bf16[70,8,1120]{2,1,0:T(8,128)(2,1)}, u32[]{:S(2)}, u32[]{:S(2)}) %collective-permute-start.14) | collective-permute-done | bytes 1254432 | tf_op jit(solution)/shard_map/ppermute | solution.py:126
  148.5 25.5 %collective-permute-done.10 = bf16[18,8,4480]{2,1,0:T(8,128)(2,1)} collective-permute-done((bf16[18,8,4480]{2,1,0:T(8,128)(2,1)}, bf16[18,8,4480]{2,1,0:T(8,128)(2,1)}, u32[]{:S(2)}, u32[]{:S(2)}) %collective-permute-start.10) | collective-permute-done | bytes 1290272 | tf_op jit(solution)/shard_map/ppermute | solution.py:126
  175.6 2.1 convolution_add_fusion.1
  180.7 11.7 %while.28 = (s32[]{:T(128)}, bf16[4,256,5,56]{1,3,2,0:T(8,128)(2,1)S(1)}, f32[4,5,256,1]{2,1,3,0:T(8,128)S(1)}, bf16[4,256,5,56]{1,3,2,0:T(8,128)(2,1)}, bf16[4,...) while((s32[]{:T(128)}, ...), condition=%wide.region_5.6_spmd.clone, body=%wide.region_2.5_spmd.clone.sunk | while | flops 76354304 | bytes 4695385 | solution.py:66
  194.2 2.7 fusion.213
  198.0 2.7 constant_dynamic-update-slice_fusion.5
  200.8 4.1 fusion.163
  212.8 8.8 %convert_reduce_fusion = (f32[4480]{0:T(1024)S(1)}, bf16[256,4480]{1,0:T(8,128)(2,1)S(1)}, bf16[256,4480]{1,0:T(8,128)(2,1)}) fusion(f32[256,2240]{1,0:T(8,128)S(1)} %get-tuple-element.203, f32[256,2240]{1,0:T(8,128)S(1)} %get-tuple-element.202, f32[4480]{0:T(1024)S(1)} %maximum_convert_fusion, f32[256,4480]{1,0:T(8,128)} %fusion.163, ...), kind=kOutput, calls=%fused_computation.88 | convolution fusion | flops 1315610240 | bytes 19389440 | tf_op jit(solution)/shard_map/dot_general | solution.py:16
  234.3 31.7 %while.29 = (s32[]{:T(128)}, bf16[4,256,5,56]{1,3,2,0:T(8,128)(2,1)}, bf16[4,256,5,56]{1,3,2,0:T(8,128)(2,1)}, bf16[4,256,5,56]{1,3,2,0:T(8,128)(2,1)}, bf16[4,2...) while((s32[]{:T(128)}, ...), condition=%wide.region_12.13_spmd.clone, body=%wide.region_10.12_spmd.clone.sunk | while | flops 187069184 | bytes 11429233 | solution.py:89
  265.9 3.0 broadcast_select_fusion.6
  269.0 4.2 fusion.150
  275.3 2.6 copy.63
  278.5 3.6 broadcast_select_fusion.33
  284.8 3.0 add_bitcast_fusion
  287.9 5.7 %fusion.128 = f32[256,1120]{0,1:T(8,128)S(1)} fusion(bf16[2240,1120]{1,0:T(8,128)(2,1)} %param.40, pred[]{:T(512)S(6)} %eq.19, bf16[256,4480]{1,0:T(8,128)(2,1)} %get-tuple-element.206), kind=kOutput, calls=%fused_computation.196 | convolution fusion | flops 1285079040 | bytes 8667137 | tf_op jit(solution)/shard_map/dot_general | solution.py:16
  299.0 5.1 fusion.95
  304.1 4.1 collective-permute-done.31
  311.5 4.4 collective-permute-done.32
  316.8 3.5 collective-permute-start.33
  329.1 6.6 %collective-permute-done.34 = bf16[140,560]{1,0:T(8,128)(2,1)S(1)} collective-permute-done((bf16[140,560]{1,0:T(8,128)(2,1)S(1)}, bf16[140,560]{1,0:T(8,128)(2,1)S(1)}, u32[]{:S(2)}, u32[]{:S(2)}) %collective-permute-start.34) | collective-permute-done | bytes 156832 | tf_op jit(solution)/shard_map/ppermute | solution.py:126
  342.2 2.4 copy.64
  344.6 2.7 fusion.151
  351.4 9.2 %collective-permute-done.21 = bf16[2,420,560]{2,0,1:T(2,128)(2,1)} collective-permute-done((bf16[2,420,560]{2,0,1:T(2,128)(2,1)}, bf16[2,420,560]{2,0,1:T(2,128)(2,1)}, u32[]{:S(2)}, u32[]{:S(2)}) %collective-permute-start.21) | collective-permute-done | bytes 940832 | tf_op jit(solution)/shard_map/ppermute | solution.py:126
  360.6 3.4 fusion.209
  365.9 3.4 fusion.210
  373.1 25.1 %collective-permute-done.22 = bf16[420,560]{1,0:T(8,128)(2,1)S(1)} collective-permute-done((bf16[420,560]{1,0:T(8,128)(2,1)S(1)}, bf16[420,560]{1,0:T(8,128)(2,1)S(1)}, u32[]{:S(2)}, u32[]{:S(2)}) %collective-permute-start.22) | collective-permute-done | bytes 470432 | tf_op jit(solution)/shard_map/ppermute | solution.py:126
  399.3 3.3 collective-permute-start.23
  405.5 4.4 broadcast_select_fusion
  419.6 11.7 %collective-permute-done.24 = bf16[420,560]{1,0:T(8,128)(2,1)S(1)} collective-permute-done((bf16[420,560]{1,0:T(8,128)(2,1)S(1)}, bf16[420,560]{1,0:T(8,128)(2,1)S(1)}, u32[]{:S(2)}, u32[]{:S(2)}) %collective-permute-start.24) | collective-permute-done | bytes 470432 | tf_op jit(solution)/shard_map/ppermute | solution.py:126
  436.4 8.4 %collective-permute-done.51 = bf16[2,140,2240]{2,0,1:T(2,128)(2,1)S(1)} collective-permute-done((bf16[2,140,2240]{2,0,1:T(2,128)(2,1)S(1)}, bf16[2,140,2240]{2,0,1:T(2,128)(2,1)S(1)}, u32[]{:S(2)}, u32[]{:S(2)}) %collective-permute-start.51) | collective-permute-done | bytes 1254432 | tf_op jit(solution)/shard_map/ppermute | solution.py:126
  448.0 15.3 %collective-permute-done.49 = bf16[2,140,2240]{2,0,1:T(2,128)(2,1)S(1)} collective-permute-done((bf16[2,140,2240]{2,0,1:T(2,128)(2,1)S(1)}, bf16[2,140,2240]{2,0,1:T(2,128)(2,1)S(1)}, u32[]{:S(2)}, u32[]{:S(2)}) %collective-permute-start.49) | collective-permute-done | bytes 1254432 | tf_op jit(solution)/shard_map/ppermute | solution.py:126
  466.6 4.2 collective-permute-start.43
  472.1 5.1 collective-permute-done.52
  479.0 3.0 collective-permute-done.50
  487.1 34.2 %collective-permute-done.44 = bf16[560,560]{1,0:T(8,128)(2,1)S(1)} collective-permute-done((bf16[560,560]{1,0:T(8,128)(2,1)S(1)}, bf16[560,560]{1,0:T(8,128)(2,1)S(1)}, u32[]{:S(2)}, u32[]{:S(2)}) %collective-permute-start.44) | collective-permute-done | bytes 627232 | tf_op jit(solution)/shard_map/ppermute | solution.py:126
  524.5 11.1 %collective-permute-done.54 = bf16[140,2240]{1,0:T(8,128)(2,1)S(1)} collective-permute-done((bf16[140,2240]{1,0:T(8,128)(2,1)S(1)}, bf16[140,2240]{1,0:T(8,128)(2,1)S(1)}, u32[]{:S(2)}, u32[]{:S(2)}) %collective-permute-start.54) | collective-permute-done | bytes 627232 | tf_op jit(solution)/shard_map/ppermute | solution.py:126
  538.0 2.1 collective-permute-start.56
  541.0 2.4 reduce_sum.218
  (408 shorter events, 180.0 us)
Async XLA Ops:
  7.2 533.8 %all-gather.4.cloned.1.call-start = ((), (), s32[]{:S(2)}) async-start(), calls=%async_computation | async-start | bytes 1774080 | tf_op jit(solution)/shard_map/all_gather | solution.py:266
  13.2 100.0 %collective-permute-start.9 = (bf16[18,8,4480]{2,1,0:T(8,128)(2,1)}, bf16[18,8,4480]{2,1,0:T(8,128)(2,1)}, u32[]{:S(2)}, u32[]{:S(2)}) collective-permute-start(bf16[18,8,4480]{2,1,0:T(8,128)(2,1)} %constant_dynamic-slice_fusion.1), channel_id=1, source_target_pairs={{0,1},{1,0},{2,3},{3,2},{4,5},{5,4},{6,7},{7,6},{8,9},{9,8},{10,11... | collective-permute-start | bytes 3870728 | tf_op jit(solution)/shard_map/ppermute | solution.py:126
  17.0 66.6 %collective-permute-start.5 = (bf16[18,8,1120]{2,1,0:T(8,128)(2,1)}, bf16[18,8,1120]{2,1,0:T(8,128)(2,1)}, u32[]{:S(2)}, u32[]{:S(2)}) collective-permute-start(bf16[18,8,1120]{2,1,0:T(8,128)(2,1)} %constant_dynamic-slice_fusion.2), channel_id=1, source_target_pairs={{0,1},{1,0},{2,3},{3,2},{4,5},{5,4},{6,7},{7,6},{8,9},{9,8},{10,11... | collective-permute-start | bytes 967688 | tf_op jit(solution)/shard_map/ppermute | solution.py:126
  19.3 74.5 %collective-permute-start.1 = (bf16[18,8,3360]{2,1,0:T(8,128)(2,1)}, bf16[18,8,3360]{2,1,0:T(8,128)(2,1)}, u32[]{:S(2)}, u32[]{:S(2)}) collective-permute-start(bf16[18,8,3360]{2,1,0:T(8,128)(2,1)} %constant_dynamic-slice_fusion.3), channel_id=1, source_target_pairs={{0,1},{1,0},{2,3},{3,2},{4,5},{5,4},{6,7},{7,6},{8,9},{9,8},{10,11... | collective-permute-start | bytes 2903048 | tf_op jit(solution)/shard_map/ppermute | solution.py:126
  21.5 52.0 %collective-permute-start = (bf16[6720]{0:T(1024)(128)(2,1)S(1)}, bf16[6720]{0:T(1024)(128)(2,1)S(1)}, u32[]{:S(2)}, u32[]{:S(2)}) collective-permute-start(bf16[6720]{0:T(1024)(128)(2,1)S(1)} %concatenate.120), channel_id=1, source_target_pairs={{0,1},{1,0},{2,3},{3,2},{4,5},{5,4},{6,7},{7,6},{8,9},{9,8},{10,11... | collective-permute-start | bytes 40328 | tf_op jit(solution)/shard_map/ppermute | solution.py:126
  22.4 57.6 %collective-permute-start.47 = (bf16[256,560]{0,1:T(8,128)(2,1)}, bf16[256,560]{0,1:T(8,128)(2,1)S(1)}, u32[]{:S(2)}, u32[]{:S(2)}) collective-permute-start(bf16[256,560]{0,1:T(8,128)(2,1)} %get-tuple-element.251), channel_id=1, source_target_pairs={{0,2},{1,3},{2,0},{3,1},{4,6},{5,7},{6,4},{7,5},{8,10},{9,11},{10,... | collective-permute-start | bytes 860168 | tf_op jit(solution)/shard_map/ppermute | solution.py:126
  80.0 30.8 %collective-permute-start.13 = (bf16[70,8,1120]{2,1,0:T(8,128)(2,1)S(1)}, bf16[70,8,1120]{2,1,0:T(8,128)(2,1)S(1)}, u32[]{:S(2)}, u32[]{:S(2)}) collective-permute-start(bf16[70,8,1120]{2,1,0:T(8,128)(2,1)S(1)} %constant_dynamic-slice_fusion), channel_id=1, source_target_pairs={{0,1},{1,0},{2,3},{3,2},{4,5},{5,4},{6,7},{7,6},{8,9},{9,8},{10,11... | collective-permute-start | bytes 3763208 | tf_op jit(solution)/shard_map/ppermute | solution.py:126
  93.8 25.2 %collective-permute-start.2 = (bf16[18,8,3360]{2,1,0:T(8,128)(2,1)}, bf16[18,8,3360]{2,1,0:T(8,128)(2,1)S(1)}, u32[]{:S(2)}, u32[]{:S(2)}) collective-permute-start(bf16[18,8,3360]{2,1,0:T(8,128)(2,1)} %collective-permute-done.1), channel_id=1, source_target_pairs={{0,4},{1,5},{2,6},{3,7},{4,0},{5,1},{6,2},{7,3},{8,12},{9,13},{10,... | collective-permute-start | bytes 2903048 | tf_op jit(solution)/shard_map/ppermute | solution.py:126
  95.4 23.7 %collective-permute-start.3 = (bf16[18,8,3360]{2,1,0:T(8,128)(2,1)}, bf16[18,8,3360]{2,1,0:T(8,128)(2,1)S(1)}, u32[]{:S(2)}, u32[]{:S(2)}) collective-permute-start(bf16[18,8,3360]{2,1,0:T(8,128)(2,1)} %collective-permute-done.1), channel_id=1, source_target_pairs={{0,2},{1,3},{2,0},{3,1},{4,6},{5,7},{6,4},{7,5},{8,10},{9,11},{10,... | collective-permute-start | bytes 2903048 | tf_op jit(solution)/shard_map/ppermute | solution.py:126
  110.8 35.9 %collective-permute-start.14 = (bf16[70,8,1120]{2,1,0:T(8,128)(2,1)S(1)}, bf16[70,8,1120]{2,1,0:T(8,128)(2,1)}, u32[]{:S(2)}, u32[]{:S(2)}) collective-permute-start(bf16[70,8,1120]{2,1,0:T(8,128)(2,1)S(1)} %collective-permute-done.13), channel_id=1, source_target_pairs={{0,4},{1,5},{2,6},{3,7},{4,0},{5,1},{6,2},{7,3},{8,12},{9,13},{10,... | collective-permute-start | bytes 3763208 | tf_op jit(solution)/shard_map/ppermute | solution.py:126
  112.6 35.7 %collective-permute-start.15 = (bf16[70,8,1120]{2,1,0:T(8,128)(2,1)S(1)}, bf16[70,8,1120]{2,1,0:T(8,128)(2,1)S(1)}, u32[]{:S(2)}, u32[]{:S(2)}) collective-permute-start(bf16[70,8,1120]{2,1,0:T(8,128)(2,1)S(1)} %collective-permute-done.13), channel_id=1, source_target_pairs={{0,2},{1,3},{2,0},{3,1},{4,6},{5,7},{6,4},{7,5},{8,10},{9,11},{10,... | collective-permute-start | bytes 3763208 | tf_op jit(solution)/shard_map/ppermute | solution.py:126
  113.2 60.8 %collective-permute-start.10 = (bf16[18,8,4480]{2,1,0:T(8,128)(2,1)}, bf16[18,8,4480]{2,1,0:T(8,128)(2,1)}, u32[]{:S(2)}, u32[]{:S(2)}) collective-permute-start(bf16[18,8,4480]{2,1,0:T(8,128)(2,1)} %collective-permute-done.9), channel_id=1, source_target_pairs={{0,4},{1,5},{2,6},{3,7},{4,0},{5,1},{6,2},{7,3},{8,12},{9,13},{10,... | collective-permute-start | bytes 3870728 | tf_op jit(solution)/shard_map/ppermute | solution.py:126
  119.0 79.1 %collective-permute-start.11 = (bf16[18,8,4480]{2,1,0:T(8,128)(2,1)}, bf16[18,8,4480]{2,1,0:T(8,128)(2,1)}, u32[]{:S(2)}, u32[]{:S(2)}) collective-permute-start(bf16[18,8,4480]{2,1,0:T(8,128)(2,1)} %collective-permute-done.9), channel_id=1, source_target_pairs={{0,2},{1,3},{2,0},{3,1},{4,6},{5,7},{6,4},{7,5},{8,10},{9,11},{10,... | collective-permute-start | bytes 3870728 | tf_op jit(solution)/shard_map/ppermute | solution.py:126
  119.1 56.3 %collective-permute-start.4 = (bf16[18,8,3360]{2,1,0:T(8,128)(2,1)S(1)}, bf16[18,8,3360]{2,1,0:T(8,128)(2,1)S(1)}, u32[]{:S(2)}, u32[]{:S(2)}) collective-permute-start(bf16[18,8,3360]{2,1,0:T(8,128)(2,1)S(1)} %collective-permute-done.2), channel_id=1, source_target_pairs={{0,2},{1,3},{2,0},{3,1},{4,6},{5,7},{6,4},{7,5},{8,10},{9,11},{10,... | collective-permute-start | bytes 2903048 | tf_op jit(solution)/shard_map/ppermute | solution.py:126
  146.7 60.6 %collective-permute-start.16 = (bf16[70,8,1120]{2,1,0:T(8,128)(2,1)}, bf16[70,8,1120]{2,1,0:T(8,128)(2,1)}, u32[]{:S(2)}, u32[]{:S(2)}) collective-permute-start(bf16[70,8,1120]{2,1,0:T(8,128)(2,1)} %collective-permute-done.14), channel_id=1, source_target_pairs={{0,2},{1,3},{2,0},{3,1},{4,6},{5,7},{6,4},{7,5},{8,10},{9,11},{10,... | collective-permute-start | bytes 3763208 | tf_op jit(solution)/shard_map/ppermute | solution.py:126
  173.9 37.4 %collective-permute-start.12 = (bf16[18,8,4480]{2,1,0:T(8,128)(2,1)}, bf16[18,8,4480]{2,1,0:T(8,128)(2,1)}, u32[]{:S(2)}, u32[]{:S(2)}) collective-permute-start(bf16[18,8,4480]{2,1,0:T(8,128)(2,1)} %collective-permute-done.10), channel_id=1, source_target_pairs={{0,2},{1,3},{2,0},{3,1},{4,6},{5,7},{6,4},{7,5},{8,10},{9,11},{10,... | collective-permute-start | bytes 3870728 | tf_op jit(solution)/shard_map/ppermute | solution.py:126
  274.7 129.2 %collective-permute-start.48 = (bf16[256,4480]{1,0:T(8,128)(2,1)}, bf16[256,4480]{1,0:T(8,128)(2,1)}, u32[]{:S(2)}, u32[]{:S(2)}) collective-permute-start(bf16[256,4480]{1,0:T(8,128)(2,1)} %get-tuple-element.206), channel_id=1, source_target_pairs={{0,2},{1,3},{2,0},{3,1},{4,6},{5,7},{6,4},{7,5},{8,10},{9,11},{10,... | collective-permute-start | bytes 6881288 | tf_op jit(solution)/shard_map/ppermute | solution.py:126
  277.8 64.3 %collective-permute-start.37 = (bf16[256,2240]{0,1:T(8,128)(2,1)}, bf16[256,2240]{0,1:T(8,128)(2,1)}, u32[]{:S(2)}, u32[]{:S(2)}) collective-permute-start(bf16[256,2240]{0,1:T(8,128)(2,1)} %copy.63), channel_id=1, source_target_pairs={{0,2},{1,3},{2,0},{3,1},{4,6},{5,7},{6,4},{7,5},{8,10},{9,11},{10,... | collective-permute-start | bytes 3440648 | tf_op jit(solution)/shard_map/ppermute | solution.py:126
  277.9 15.7 %collective-permute-start.27 = (bf16[256,560]{0,1:T(8,128)(2,1)}, bf16[256,560]{0,1:T(8,128)(2,1)}, u32[]{:S(2)}, u32[]{:S(2)}) collective-permute-start(bf16[256,560]{0,1:T(8,128)(2,1)} %get-tuple-element.257), channel_id=1, source_target_pairs={{0,2},{1,3},{2,0},{3,1},{4,6},{5,7},{6,4},{7,5},{8,10},{9,11},{10,... | collective-permute-start | bytes 860168 | tf_op jit(solution)/shard_map/ppermute | solution.py:126
  278.4 43.2 %collective-permute-start.17 = (bf16[256,1680]{0,1:T(8,128)(2,1)}, bf16[256,1680]{0,1:T(8,128)(2,1)}, u32[]{:S(2)}, u32[]{:S(2)}) collective-permute-start(bf16[256,1680]{0,1:T(8,128)(2,1)} %get-tuple-element.225), channel_id=1, source_target_pairs={{0,2},{1,3},{2,0},{3,1},{4,6},{5,7},{6,4},{7,5},{8,10},{9,11},{10,... | collective-permute-start | bytes 2580488 | tf_op jit(solution)/shard_map/ppermute | solution.py:126
  295.6 14.0 %collective-permute-start.29 = (bf16[2,140,560]{2,1,0:T(8,128)(2,1)S(1)}, bf16[2,140,560]{2,1,0:T(8,128)(2,1)S(1)}, u32[]{:S(2)}, u32[]{:S(2)}) collective-permute-start(bf16[2,140,560]{2,1,0:T(8,128)(2,1)S(1)} %pad_maximum_fusion.20), channel_id=1, source_target_pairs={{0,1},{1,0},{2,3},{3,2},{4,5},{5,4},{6,7},{7,6},{8,9},{9,8},{10,11... | collective-permute-start | bytes 940808 | tf_op jit(solution)/shard_map/ppermute | solution.py:126
  297.4 10.7 %collective-permute-start.31 = (bf16[2,140,560]{2,1,0:T(8,128)(2,1)S(1)}, bf16[2,140,560]{2,1,0:T(8,128)(2,1)S(1)}, u32[]{:S(2)}, u32[]{:S(2)}) collective-permute-start(bf16[2,140,560]{2,1,0:T(8,128)(2,1)S(1)} %pad_maximum_fusion.21), channel_id=1, source_target_pairs={{0,4},{1,5},{2,6},{3,7},{4,0},{5,1},{6,2},{7,3},{8,12},{9,13},{10,... | collective-permute-start | bytes 940808 | tf_op jit(solution)/shard_map/ppermute | solution.py:126
  316.8 11.3 %collective-permute-start.33 = (bf16[140,560]{1,0:T(8,128)(2,1)S(1)}, bf16[140,560]{1,0:T(8,128)(2,1)S(1)}, u32[]{:S(2)}, u32[]{:S(2)}) collective-permute-start(bf16[140,560]{1,0:T(8,128)(2,1)S(1)} %get-tuple-element.246), channel_id=1, source_target_pairs={{0,8},{1,9},{4,12},{5,13},{8,0},{9,1},{12,4},{13,5},{18,26},{19,27... | collective-permute-start | bytes 470408 | tf_op jit(solution)/shard_map/ppermute | solution.py:126
  320.3 15.4 %collective-permute-start.35 = (bf16[140,560]{1,0:T(8,128)(2,1)S(1)}, bf16[140,560]{1,0:T(8,128)(2,1)S(1)}, u32[]{:S(2)}, u32[]{:S(2)}) collective-permute-start(bf16[140,560]{1,0:T(8,128)(2,1)S(1)} %get-tuple-element.246), channel_id=1, source_target_pairs={{2,26},{3,27},{6,30},{7,31},{10,18},{11,19},{14,22},{15,23},{16,8}... | collective-permute-start | bytes 470408 | tf_op jit(solution)/shard_map/ppermute | solution.py:126
  321.6 14.1 %collective-permute-start.34 = (bf16[140,560]{1,0:T(8,128)(2,1)S(1)}, bf16[140,560]{1,0:T(8,128)(2,1)S(1)}, u32[]{:S(2)}, u32[]{:S(2)}) collective-permute-start(bf16[140,560]{1,0:T(8,128)(2,1)S(1)} %get-tuple-element.245), channel_id=1, source_target_pairs={{2,18},{3,19},{6,22},{7,23},{10,26},{11,27},{14,30},{15,31},{16,0}... | collective-permute-start | bytes 470408 | tf_op jit(solution)/shard_map/ppermute | solution.py:126
  328.1 37.7 %collective-permute-start.19 = (bf16[2,420,560]{2,0,1:T(2,128)(2,1)}, bf16[2,420,560]{2,0,1:T(2,128)(2,1)}, u32[]{:S(2)}, u32[]{:S(2)}) collective-permute-start(bf16[2,420,560]{2,0,1:T(2,128)(2,1)} %copy.57), channel_id=1, source_target_pairs={{0,1},{1,0},{2,3},{3,2},{4,5},{5,4},{6,7},{7,6},{8,9},{9,8},{10,11... | collective-permute-start | bytes 2822408 | tf_op jit(solution)/shard_map/ppermute | solution.py:126
  340.1 20.5 %collective-permute-start.21 = (bf16[2,420,560]{2,0,1:T(2,128)(2,1)}, bf16[2,420,560]{2,0,1:T(2,128)(2,1)}, u32[]{:S(2)}, u32[]{:S(2)}) collective-permute-start(bf16[2,420,560]{2,0,1:T(2,128)(2,1)} %copy.60), channel_id=1, source_target_pairs={{0,4},{1,5},{2,6},{3,7},{4,0},{5,1},{6,2},{7,3},{8,12},{9,13},{10,... | collective-permute-start | bytes 2822408 | tf_op jit(solution)/shard_map/ppermute | solution.py:126
  349.1 67.5 %collective-permute-start.39 = (bf16[2,560,560]{2,1,0:T(8,128)(2,1)S(1)}, bf16[2,560,560]{2,1,0:T(8,128)(2,1)S(1)}, u32[]{:S(2)}, u32[]{:S(2)}) collective-permute-start(bf16[2,560,560]{2,1,0:T(8,128)(2,1)S(1)} %pad_maximum_fusion.3), channel_id=1, source_target_pairs={{0,1},{1,0},{2,3},{3,2},{4,5},{5,4},{6,7},{7,6},{8,9},{9,8},{10,11... | collective-permute-start | bytes 3763208 | tf_op jit(solution)/shard_map/ppermute | solution.py:126
  364.5 33.6 %collective-permute-start.22 = (bf16[420,560]{1,0:T(8,128)(2,1)S(1)}, bf16[420,560]{1,0:T(8,128)(2,1)S(1)}, u32[]{:S(2)}, u32[]{:S(2)}) collective-permute-start(bf16[420,560]{1,0:T(8,128)(2,1)S(1)} %fusion.111), channel_id=1, source_target_pairs={{0,1},{1,0},{2,3},{3,2},{4,5},{5,4},{6,7},{7,6},{8,9},{9,8},{10,11... | collective-permute-start | bytes 1411208 | tf_op jit(solution)/shard_map/ppermute | solution.py:126
  369.9 28.8 %collective-permute-start.20 = (bf16[420,560]{1,0:T(8,128)(2,1)S(1)}, bf16[420,560]{1,0:T(8,128)(2,1)S(1)}, u32[]{:S(2)}, u32[]{:S(2)}) collective-permute-start(bf16[420,560]{1,0:T(8,128)(2,1)S(1)} %fusion.110), channel_id=1, source_target_pairs={{0,4},{1,5},{2,6},{3,7},{4,0},{5,1},{6,2},{7,3},{8,12},{9,13},{10,... | collective-permute-start | bytes 1411208 | tf_op jit(solution)/shard_map/ppermute | solution.py:126
  372.2 42.1 %collective-permute-start.41 = (bf16[2,560,560]{2,1,0:T(8,128)(2,1)S(1)}, bf16[2,560,560]{2,1,0:T(8,128)(2,1)S(1)}, u32[]{:S(2)}, u32[]{:S(2)}) collective-permute-start(bf16[2,560,560]{2,1,0:T(8,128)(2,1)S(1)} %pad_maximum_fusion.4), channel_id=1, source_target_pairs={{0,4},{1,5},{2,6},{3,7},{4,0},{5,1},{6,2},{7,3},{8,12},{9,13},{10,... | collective-permute-start | bytes 3763208 | tf_op jit(solution)/shard_map/ppermute | solution.py:126
  399.3 18.8 %collective-permute-start.23 = (bf16[420,560]{1,0:T(8,128)(2,1)S(1)}, bf16[420,560]{1,0:T(8,128)(2,1)S(1)}, u32[]{:S(2)}, u32[]{:S(2)}) collective-permute-start(bf16[420,560]{1,0:T(8,128)(2,1)S(1)} %get-tuple-element.220), channel_id=1, source_target_pairs={{0,8},{1,9},{4,12},{5,13},{8,0},{9,1},{12,4},{13,5},{18,26},{19,27... | collective-permute-start | bytes 1411208 | tf_op jit(solution)/shard_map/ppermute | solution.py:126
  402.6 30.4 %collective-permute-start.25 = (bf16[420,560]{1,0:T(8,128)(2,1)S(1)}, bf16[420,560]{1,0:T(8,128)(2,1)S(1)}, u32[]{:S(2)}, u32[]{:S(2)}) collective-permute-start(bf16[420,560]{1,0:T(8,128)(2,1)S(1)} %get-tuple-element.220), channel_id=1, source_target_pairs={{2,26},{3,27},{6,30},{7,31},{10,18},{11,19},{14,22},{15,23},{16,8}... | collective-permute-start | bytes 1411208 | tf_op jit(solution)/shard_map/ppermute | solution.py:126
  403.9 27.5 %collective-permute-start.24 = (bf16[420,560]{1,0:T(8,128)(2,1)S(1)}, bf16[420,560]{1,0:T(8,128)(2,1)S(1)}, u32[]{:S(2)}, u32[]{:S(2)}) collective-permute-start(bf16[420,560]{1,0:T(8,128)(2,1)S(1)} %get-tuple-element.219), channel_id=1, source_target_pairs={{2,18},{3,19},{6,22},{7,23},{10,26},{11,27},{14,30},{15,31},{16,0}... | collective-permute-start | bytes 1411208 | tf_op jit(solution)/shard_map/ppermute | solution.py:126
  414.3 30.5 %collective-permute-start.51 = (bf16[2,140,2240]{2,0,1:T(2,128)(2,1)S(1)}, bf16[2,140,2240]{2,0,1:T(2,128)(2,1)S(1)}, u32[]{:S(2)}, u32[]{:S(2)}) collective-permute-start(bf16[2,140,2240]{2,0,1:T(2,128)(2,1)S(1)} %copy.68), channel_id=1, source_target_pairs={{0,4},{1,5},{2,6},{3,7},{4,0},{5,1},{6,2},{7,3},{8,12},{9,13},{10,... | collective-permute-start | bytes 3763208 | tf_op jit(solution)/shard_map/ppermute | solution.py:126
  416.7 19.0 %collective-permute-start.42 = (bf16[560,560]{1,0:T(8,128)(2,1)S(1)}, bf16[560,560]{1,0:T(8,128)(2,1)S(1)}, u32[]{:S(2)}, u32[]{:S(2)}) collective-permute-start(bf16[560,560]{1,0:T(8,128)(2,1)S(1)} %fusion.109), channel_id=1, source_target_pairs={{0,1},{1,0},{2,3},{3,2},{4,5},{5,4},{6,7},{7,6},{8,9},{9,8},{10,11... | collective-permute-start | bytes 1881608 | tf_op jit(solution)/shard_map/ppermute | solution.py:126
  418.1 45.2 %collective-permute-start.49 = (bf16[2,140,2240]{2,0,1:T(2,128)(2,1)S(1)}, bf16[2,140,2240]{2,0,1:T(2,128)(2,1)S(1)}, u32[]{:S(2)}, u32[]{:S(2)}) collective-permute-start(bf16[2,140,2240]{2,0,1:T(2,128)(2,1)S(1)} %copy.65), channel_id=1, source_target_pairs={{0,1},{1,0},{2,3},{3,2},{4,5},{5,4},{6,7},{7,6},{8,9},{9,8},{10,11... | collective-permute-start | bytes 3763208 | tf_op jit(solution)/shard_map/ppermute | solution.py:126
  431.4 34.4 %collective-permute-start.40 = (bf16[560,560]{1,0:T(8,128)(2,1)S(1)}, bf16[560,560]{1,0:T(8,128)(2,1)S(1)}, u32[]{:S(2)}, u32[]{:S(2)}) collective-permute-start(bf16[560,560]{1,0:T(8,128)(2,1)S(1)} %fusion.108), channel_id=1, source_target_pairs={{0,4},{1,5},{2,6},{3,7},{4,0},{5,1},{6,2},{7,3},{8,12},{9,13},{10,... | collective-permute-start | bytes 1881608 | tf_op jit(solution)/shard_map/ppermute | solution.py:126
  433.3 106.8 %collective-permute-start.26 = (f32[210,560]{1,0:T(8,128)S(1)}, f32[210,560]{1,0:T(8,128)S(1)}, u32[]{:S(2)}, u32[]{:S(2)}) collective-permute-start(f32[210,560]{1,0:T(8,128)S(1)} %slice_select_fusion.2), channel_id=1, source_target_pairs={{0,2},{1,3},{4,6},{5,7},{8,10},{9,11},{12,14},{13,15},{18,16},{19,... | collective-permute-start | bytes 1411208 | tf_op jit(solution)/shard_map/ppermute | solution.py:126
  447.1 30.1 %collective-permute-start.52 = (bf16[140,2240]{1,0:T(8,128)(2,1)S(1)}, bf16[140,2240]{1,0:T(8,128)(2,1)S(1)}, u32[]{:S(2)}, u32[]{:S(2)}) collective-permute-start(bf16[140,2240]{1,0:T(8,128)(2,1)S(1)} %fusion.76), channel_id=1, source_target_pairs={{0,1},{1,0},{2,3},{3,2},{4,5},{5,4},{6,7},{7,6},{8,9},{9,8},{10,11... | collective-permute-start | bytes 1881608 | tf_op jit(solution)/shard_map/ppermute | solution.py:126
  465.6 16.4 %collective-permute-start.50 = (bf16[140,2240]{1,0:T(8,128)(2,1)S(1)}, bf16[140,2240]{1,0:T(8,128)(2,1)S(1)}, u32[]{:S(2)}, u32[]{:S(2)}) collective-permute-start(bf16[140,2240]{1,0:T(8,128)(2,1)S(1)} %fusion.75), channel_id=1, source_target_pairs={{0,4},{1,5},{2,6},{3,7},{4,0},{5,1},{6,2},{7,3},{8,12},{9,13},{10,... | collective-permute-start | bytes 1881608 | tf_op jit(solution)/shard_map/ppermute | solution.py:126
  466.6 19.3 %collective-permute-start.43 = (bf16[560,560]{1,0:T(8,128)(2,1)S(1)}, bf16[560,560]{1,0:T(8,128)(2,1)S(1)}, u32[]{:S(2)}, u32[]{:S(2)}) collective-permute-start(bf16[560,560]{1,0:T(8,128)(2,1)S(1)} %get-tuple-element.210), channel_id=1, source_target_pairs={{0,8},{1,9},{4,12},{5,13},{8,0},{9,1},{12,4},{13,5},{18,26},{19,27... | collective-permute-start | bytes 1881608 | tf_op jit(solution)/shard_map/ppermute | solution.py:126
  470.8 51.9 %collective-permute-start.45 = (bf16[560,560]{1,0:T(8,128)(2,1)S(1)}, bf16[560,560]{1,0:T(8,128)(2,1)S(1)}, u32[]{:S(2)}, u32[]{:S(2)}) collective-permute-start(bf16[560,560]{1,0:T(8,128)(2,1)S(1)} %get-tuple-element.210), channel_id=1, source_target_pairs={{2,26},{3,27},{6,30},{7,31},{10,18},{11,19},{14,22},{15,23},{16,8}... | collective-permute-start | bytes 1881608 | tf_op jit(solution)/shard_map/ppermute | solution.py:126
  477.2 44.2 %collective-permute-start.44 = (bf16[560,560]{1,0:T(8,128)(2,1)S(1)}, bf16[560,560]{1,0:T(8,128)(2,1)S(1)}, u32[]{:S(2)}, u32[]{:S(2)}) collective-permute-start(bf16[560,560]{1,0:T(8,128)(2,1)S(1)} %get-tuple-element.209), channel_id=1, source_target_pairs={{2,18},{3,19},{6,22},{7,23},{10,26},{11,27},{14,30},{15,31},{16,0}... | collective-permute-start | bytes 1881608 | tf_op jit(solution)/shard_map/ppermute | solution.py:126
  482.7 41.8 %collective-permute-start.53 = (bf16[140,2240]{1,0:T(8,128)(2,1)S(1)}, bf16[140,2240]{1,0:T(8,128)(2,1)S(1)}, u32[]{:S(2)}, u32[]{:S(2)}) collective-permute-start(bf16[140,2240]{1,0:T(8,128)(2,1)S(1)} %get-tuple-element.212), channel_id=1, source_target_pairs={{0,8},{1,9},{4,12},{5,13},{8,0},{9,1},{12,4},{13,5},{18,26},{19,27... | collective-permute-start | bytes 1881608 | tf_op jit(solution)/shard_map/ppermute | solution.py:126
  485.8 49.8 %collective-permute-start.55 = (bf16[140,2240]{1,0:T(8,128)(2,1)S(1)}, bf16[140,2240]{1,0:T(8,128)(2,1)S(1)}, u32[]{:S(2)}, u32[]{:S(2)}) collective-permute-start(bf16[140,2240]{1,0:T(8,128)(2,1)S(1)} %get-tuple-element.212), channel_id=1, source_target_pairs={{2,26},{3,27},{6,30},{7,31},{10,18},{11,19},{14,22},{15,23},{16,8}... | collective-permute-start | bytes 1881608 | tf_op jit(solution)/shard_map/ppermute | solution.py:126
  521.4 14.2 %collective-permute-start.54 = (bf16[140,2240]{1,0:T(8,128)(2,1)S(1)}, bf16[140,2240]{1,0:T(8,128)(2,1)S(1)}, u32[]{:S(2)}, u32[]{:S(2)}) collective-permute-start(bf16[140,2240]{1,0:T(8,128)(2,1)S(1)} %get-tuple-element.211), channel_id=1, source_target_pairs={{2,18},{3,19},{6,22},{7,23},{10,26},{11,27},{14,30},{15,31},{16,0}... | collective-permute-start | bytes 1881608 | tf_op jit(solution)/shard_map/ppermute | solution.py:126
  523.2 21.7 %collective-permute-start.46 = (f32[280,560]{1,0:T(8,128)S(1)}, f32[280,560]{1,0:T(8,128)S(1)}, u32[]{:S(2)}, u32[]{:S(2)}) collective-permute-start(f32[280,560]{1,0:T(8,128)S(1)} %slice_select_fusion), channel_id=1, source_target_pairs={{0,2},{1,3},{4,6},{5,7},{8,10},{9,11},{12,14},{13,15},{18,16},{19,... | collective-permute-start | bytes 1881608 | tf_op jit(solution)/shard_map/ppermute | solution.py:126
  (69 other events, 437.3 us)
Sparse Core Ops, SparseCore 0:
  284.9 58.4 all-gather.3
